TPU v7x, 512 devices: a whole 4x8x8 slice. The times are simulated.
512 devices in a mesh: grp: 8 (over y), exp: 64 (over x, z, core).
Axes of the slice: x: 4, y: 8, z: 8, core: 2. Of those that a mesh axis runs over, the one named last changes fastest.
Arguments:
- tokens: bfloat16 [65536, 1024], P(('grp', 'exp')), may hold values from -6 to 6
- w_in: bfloat16 [128, 1024, 768], P('exp', 'grp'), may hold values from -0.1875 to 0.1875
- w_out: bfloat16 [128, 384, 1024], P('exp', 'grp'), may hold values from -0.3125 to 0.3125
- moments_in: bfloat16 [128, 2, 1024, 768], P('exp', None, 'grp'), may hold values from -6 to 6
- moments_out: bfloat16 [128, 2, 384, 1024], P('exp', None, 'grp'), may hold values from -6 to 6
- expert_ids: int32 [65536, 8], P(('grp', 'exp')), may hold values from 0 to 95, all different within a row; in each aligned block of 128 rows (0 to 127, 128 to 255, ...) at most 16 rows name the same one
- route_weights: float32 [65536, 8], P(('grp', 'exp')), may hold values from 0.1 to 1
- old_plan: int32 [128], replicated, may hold values from 0 to 95, as said below
- new_plan: int32 [128], replicated, may hold values from 0 to 95, as said below
Outputs:
- mixed: bfloat16 [65536, 1024], P(('grp', 'exp'))
- new_w_in: bfloat16 [128, 1024, 768], P('exp', 'grp')
- new_w_out: bfloat16 [128, 384, 1024], P('exp', 'grp')
- new_moments_in: bfloat16 [128, 2, 1024, 768], P('exp', None, 'grp')
- new_moments_out: bfloat16 [128, 2, 384, 1024], P('exp', None, 'grp')
Inputs may be any that keep to these rules, and one draw needn't show every extreme that they name: `expert_ids`: each row names 8 different experts. Among the rows of one device no expert is named more than 16 times, and in every draw some device names some expert exactly 16 times. `old_plan`: every expert is held by one or two slots; exactly 32 experts are held by two. `new_plan`: every expert is held by one or two slots; exactly 32 experts are held by two.
All inputs are finite; a program needn't handle non-finite values.
Results may differ from a plain program's by a relative error of at most 0.0057.
Values may be sent and summed in bfloat16 or wider, within the bound.
A program may use at most 64 MiB of HBM per device.

v0:
```python
import jax
import jax.numpy as jnp
from jax import lax
from jax.sharding import PartitionSpec as P

TOP = 8
TOK_DEV = 128


def on_device(
    tokens, w_in, w_out, moments_in, moments_out, expert_ids, route_weights, old_plan, new_plan
):
    device_count = lax.axis_size("exp")
    per_device = w_in.shape[0]
    slot_count = per_device * device_count
    expert_count = 3 * device_count // 2
    capacity = 3 * TOK_DEV * TOP // (2 * expert_count)
    width = tokens.shape[1]
    token_count = tokens.shape[0]
    slot_index = jnp.arange(slot_count, dtype=jnp.int32)
    same_expert = new_plan[:, None] == old_plan[None, :]
    source = jnp.min(jnp.where(same_expert, slot_index[None, :], slot_count), axis=1)
    flat_in = w_in.reshape(per_device, -1)
    flat_out = w_out.reshape(per_device, -1)
    flat_moments_in = moments_in.reshape(per_device, -1)
    flat_moments_out = moments_out.reshape(per_device, -1)
    spread = (
        lax.all_to_all(flat_in, "exp", split_axis=1, concat_axis=0, tiled=True),
        lax.all_to_all(flat_out, "exp", split_axis=1, concat_axis=0, tiled=True),
        lax.all_to_all(flat_moments_in, "exp", split_axis=1, concat_axis=0, tiled=True),
        lax.all_to_all(flat_moments_out, "exp", split_axis=1, concat_axis=0, tiled=True),
    )
    picked = tuple((jnp.take(piece, source, axis=0) for piece in spread))
    landed = (
        lax.all_to_all(picked[0], "exp", split_axis=0, concat_axis=1, tiled=True),
        lax.all_to_all(picked[1], "exp", split_axis=0, concat_axis=1, tiled=True),
        lax.all_to_all(picked[2], "exp", split_axis=0, concat_axis=1, tiled=True),
        lax.all_to_all(picked[3], "exp", split_axis=0, concat_axis=1, tiled=True),
    )
    new_w_in = landed[0].reshape(w_in.shape)
    new_w_out = landed[1].reshape(w_out.shape)
    new_moments_in = landed[2].reshape(moments_in.shape)
    new_moments_out = landed[3].reshape(moments_out.shape)
    full_in, full_out = (
        lax.all_gather(new_w_in, "grp", axis=1, tiled=True),
        lax.all_gather(new_w_out, "grp", axis=1, tiled=True),
    )
    hidden_size = full_out.shape[1]
    pair_count = token_count * TOP
    pair_expert = expert_ids.reshape(-1)
    expert_index = jnp.arange(expert_count, dtype=jnp.int32)
    holders = new_plan[None, :] == expert_index[:, None]
    first_slot = jnp.min(jnp.where(holders, slot_index[None, :], slot_count), axis=1)
    chosen = pair_expert[:, None] == expert_index[None, :]
    pair_first = jnp.sum(jnp.where(chosen, first_slot[None, :], 0), axis=1)
    onehot = (pair_first[:, None] == slot_index[None, :]).astype(jnp.int32)
    running = jnp.cumsum(onehot, axis=0)
    position = jnp.sum(onehot * running, axis=1) - 1
    target = pair_first * capacity + position
    pair_token = jnp.arange(pair_count, dtype=jnp.int32) // TOP
    outgoing = (
        jnp.zeros((slot_count * capacity, width), jnp.bfloat16).at[target].set(tokens[pair_token])
    )
    outgoing = outgoing.reshape(device_count, per_device, capacity, width)
    both = jnp.einsum(
        "njcd,jdh->njch",
        lax.all_to_all(outgoing, "exp", split_axis=0, concat_axis=0, tiled=True),
        full_in,
        preferred_element_type=jnp.float32,
    )
    hidden = (jax.nn.silu(both[..., :hidden_size]) * both[..., hidden_size:]).astype(jnp.bfloat16)
    result = jnp.einsum(
        "njch,jhd->njcd", hidden, full_out, preferred_element_type=jnp.float32
    ).astype(jnp.bfloat16)
    returned = lax.all_to_all(result, "exp", split_axis=0, concat_axis=0, tiled=True)
    returned = returned.reshape(slot_count * capacity, width)
    gathered = jnp.take(returned, target, axis=0).reshape(token_count, TOP, width)
    share = route_weights / jnp.sum(route_weights, axis=1, keepdims=True)
    mixed = jnp.sum(share[:, :, None] * gathered.astype(jnp.float32), axis=1).astype(jnp.bfloat16)
    return (mixed, new_w_in, new_w_out, new_moments_in, new_moments_out)


def solution(mesh):
    return jax.shard_map(
        on_device,
        mesh=mesh,
        in_specs=(
            P(("grp", "exp"), None),
            P("exp", "grp", None),
            P("exp", "grp", None),
            P("exp", None, "grp", None),
            P("exp", None, "grp", None),
            P(("grp", "exp"), None),
            P(("grp", "exp"), None),
            P(),
            P(),
        ),
        out_specs=(
            P(("grp", "exp"), None),
            P("exp", "grp", None),
            P("exp", "grp", None),
            P("exp", None, "grp", None),
            P("exp", None, "grp", None),
        ),
        check_vma=False,
    )
```

profile of v0, /device:TPU:1, one launch (start us, length us, event | category | flops | bytes accessed | tf_op | source)
XLA Modules:
  0.0 427.5 jit_solution(1475960302296091123)
XLA Ops:
  7.2 1.2 all_to_all.106
  8.4 0.9 copy.57
  9.2 14.8 %all-to-all-start = ((bf16[2,64,768]{2,0,1:T(2,128)(2,1)}), bf16[2,64,768]{2,0,1:T(2,128)(2,1)S(1)}, u32[]{:S(2)}, u32[]{:S(2)}) async-start(bf16[2,64,768]{2,0,1:T(2,128)(2,1)} %copy.57), calls=%async_computation | async-start | bytes 393216 | tf_op jit(solution)/shard_map/all_to_all | solution.py:29
  24.1 1.1 all_to_all.112
  25.2 1.2 copy.59
  26.4 8.7 %all-to-all-done = bf16[2,64,768]{2,0,1:T(2,128)(2,1)S(1)} async-done(((bf16[2,64,768]{2,0,1:T(2,128)(2,1)}), bf16[2,64,768]{2,0,1:T(2,128)(2,1)S(1)}, u32[]{:S(2)}, u32[]{:S(2)}) %all-to-all-start) | async-done | bytes 196640 | tf_op jit(solution)/shard_map/all_to_all | solution.py:29
  35.0 5.7 %all-to-all-start.2 = ((bf16[2,64,1536]{2,0,1:T(2,128)(2,1)}), bf16[2,64,1536]{2,0,1:T(2,128)(2,1)S(1)}, u32[]{:S(2)}, u32[]{:S(2)}) async-start(bf16[2,64,1536]{2,0,1:T(2,128)(2,1)} %copy.59), calls=%async_computation.2 | async-start | bytes 786432 | tf_op jit(solution)/shard_map/all_to_all | solution.py:28
  40.7 0.2 all_to_all.127
  41.0 1.2 copy.65
  42.1 0.2 select_reduce_fusion.1
  42.3 0.1 reduce_min.24
  42.5 12.8 %all-to-all-done.2 = bf16[2,64,1536]{2,0,1:T(2,128)(2,1)S(1)} async-done(((bf16[2,64,1536]{2,0,1:T(2,128)(2,1)}), bf16[2,64,1536]{2,0,1:T(2,128)(2,1)S(1)}, u32[]{:S(2)}, u32[]{:S(2)}) %all-to-all-start.2) | async-done | bytes 393248 | tf_op jit(solution)/shard_map/all_to_all | solution.py:28
  55.2 6.2 %all-to-all-start.8 = ((bf16[2,64,1536]{2,0,1:T(2,128)(2,1)}), bf16[2,64,1536]{2,0,1:T(2,128)(2,1)S(1)}, u32[]{:S(2)}, u32[]{:S(2)}) async-start(bf16[2,64,1536]{2,0,1:T(2,128)(2,1)} %copy.65), calls=%async_computation.8 | async-start | bytes 786432 | tf_op jit(solution)/shard_map/all_to_all | solution.py:31
  61.6 0.9 gather_fusion
  62.5 0.1 gather.25
  62.6 1.0 broadcast_select_fusion.3
  63.5 0.1 all_to_all.115
  63.7 12.4 %all-to-all-done.8 = bf16[2,64,1536]{2,0,1:T(2,128)(2,1)S(1)} async-done(((bf16[2,64,1536]{2,0,1:T(2,128)(2,1)}), bf16[2,64,1536]{2,0,1:T(2,128)(2,1)S(1)}, u32[]{:S(2)}, u32[]{:S(2)}) %all-to-all-start.8) | async-done | bytes 393248 | tf_op jit(solution)/shard_map/all_to_all | solution.py:31
  76.0 6.2 %all-to-all-start.1 = ((bf16[64,2,768]{2,1,0:T(2,128)(2,1)}), bf16[64,2,768]{2,1,0:T(2,128)(2,1)S(1)}, u32[]{:S(2)}, u32[]{:S(2)}) async-start(bf16[64,2,768]{2,1,0:T(2,128)(2,1)} %broadcast_select_fusion.3), calls=%async_computation.1 | async-start | bytes 393216 | tf_op jit(solution)/shard_map/all_to_all | solution.py:36
  82.3 0.1 all_to_all.130
  82.4 0.9 gather_fusion.3
  83.3 0.9 gather_fusion.4
  84.3 0.1 broadcast_select_fusion.1
  84.4 0.9 all_to_all.116
  85.3 7.9 %all-to-all-done.1 = bf16[64,2,768]{2,1,0:T(2,128)(2,1)S(1)} async-done(((bf16[64,2,768]{2,1,0:T(2,128)(2,1)}), bf16[64,2,768]{2,1,0:T(2,128)(2,1)S(1)}, u32[]{:S(2)}, u32[]{:S(2)}) %all-to-all-start.1) | async-done | bytes 196640 | tf_op jit(solution)/shard_map/all_to_all | solution.py:36
  93.2 5.7 %all-to-all-start.3 = ((bf16[64,2,1536]{2,1,0:T(2,128)(2,1)}), bf16[64,2,1536]{2,1,0:T(2,128)(2,1)S(1)}, u32[]{:S(2)}, u32[]{:S(2)}) async-start(bf16[64,2,1536]{2,1,0:T(2,128)(2,1)} %all_to_all.116), calls=%async_computation.3 | async-start | bytes 786432 | tf_op jit(solution)/shard_map/all_to_all | solution.py:35
  98.9 0.9 all_to_all.131
  99.8 13.7 %all-to-all-done.3 = bf16[64,2,1536]{2,1,0:T(2,128)(2,1)S(1)} async-done(((bf16[64,2,1536]{2,1,0:T(2,128)(2,1)}), bf16[64,2,1536]{2,1,0:T(2,128)(2,1)S(1)}, u32[]{:S(2)}, u32[]{:S(2)}) %all-to-all-start.3) | async-done | bytes 393248 | tf_op jit(solution)/shard_map/all_to_all | solution.py:35
  113.5 6.2 %all-to-all-start.9 = ((bf16[64,2,1536]{2,1,0:T(2,128)(2,1)}), bf16[64,2,1536]{2,1,0:T(2,128)(2,1)S(1)}, u32[]{:S(2)}, u32[]{:S(2)}) async-start(bf16[64,2,1536]{2,1,0:T(2,128)(2,1)} %all_to_all.131), calls=%async_computation.9 | async-start | bytes 786432 | tf_op jit(solution)/shard_map/all_to_all | solution.py:38
  119.7 0.1 copy.54
  119.8 0.1 eq.64
  119.9 0.1 select_reduce_fusion.2
  120.0 0.1 select_reduce_fusion
  120.2 0.1 copy.55
  120.3 0.5 all_to_all.121
  120.7 1.7 copy.63
  122.4 11.8 %all-to-all-done.9 = bf16[64,2,1536]{2,1,0:T(2,128)(2,1)S(1)} async-done(((bf16[64,2,1536]{2,1,0:T(2,128)(2,1)}), bf16[64,2,1536]{2,1,0:T(2,128)(2,1)S(1)}, u32[]{:S(2)}, u32[]{:S(2)}) %all-to-all-start.9) | async-done | bytes 393248 | tf_op jit(solution)/shard_map/all_to_all | solution.py:38
  134.3 6.5 %all-to-all-start.6 = ((bf16[2,64,3072]{2,0,1:T(2,128)(2,1)}), bf16[2,64,3072]{2,0,1:T(2,128)(2,1)S(1)}, u32[]{:S(2)}, u32[]{:S(2)}) async-start(bf16[2,64,3072]{2,0,1:T(2,128)(2,1)} %copy.63), calls=%async_computation.6 | async-start | bytes 1572864 | tf_op jit(solution)/shard_map/all_to_all | solution.py:30
  140.8 0.2 fusion.16
  141.1 0.1 copy.56
  141.2 0.4 fusion.15
  141.6 15.3 %scatter_custom_fusion = bf16[2048,1024]{1,0:T(8,128)(2,1)} fusion(s32[1024]{0:T(1024)S(1)} %bitcast.61, bf16[128,1024]{1,0:T(8,128)(2,1)S(1)} %copy-done, s32[1024]{0:T(1024)S(1)} %broadcast_clamp_fusion.1, bf16[]{:T(256)} %constant.86.clone.1), kind=kCustom, calls=%fused_computation.16 | custom fusion | bytes 4194306 | tf_op jit(solution)/shard_map/scatter | solution.py:62
  156.9 6.8 %all-to-all-done.6 = bf16[2,64,3072]{2,0,1:T(2,128)(2,1)S(1)} async-done(((bf16[2,64,3072]{2,0,1:T(2,128)(2,1)}), bf16[2,64,3072]{2,0,1:T(2,128)(2,1)S(1)}, u32[]{:S(2)}, u32[]{:S(2)}) %all-to-all-start.6) | async-done | bytes 786464 | tf_op jit(solution)/shard_map/all_to_all | solution.py:30
  163.7 6.5 %all-to-all-start.4 = ((bf16[64,2,16,1024]{3,2,1,0:T(8,128)(2,1)}), bf16[64,2,16,1024]{3,2,1,0:T(8,128)(2,1)}, u32[]{:S(2)}, u32[]{:S(2)}) async-start(bf16[64,2,16,1024]{3,2,1,0:T(8,128)(2,1)} %bitcast.50), calls=%async_computation.4 | async-start | bytes 8388608 | tf_op jit(solution)/shard_map/all_to_all | solution.py:67
  170.3 0.9 reshape.216
  171.3 0.8 reshape.215
  172.2 0.3 all_to_all.124
  172.5 1.0 gather_fusion.2
  173.5 0.3 gather.30
  173.9 1.7 broadcast_select_fusion
  175.6 90.5 %all-to-all-done.4 = bf16[64,2,16,1024]{3,2,1,0:T(8,128)(2,1)} async-done(((bf16[64,2,16,1024]{3,2,1,0:T(8,128)(2,1)}), bf16[64,2,16,1024]{3,2,1,0:T(8,128)(2,1)}, u32[]{:S(2)}, u32[]{:S(2)}) %all-to-all-start.4) | async-done | bytes 4194336 | tf_op jit(solution)/shard_map/all_to_all | solution.py:67
  266.1 14.5 %all-to-all-start.7 = ((bf16[64,2,3072]{2,1,0:T(2,128)(2,1)}), bf16[64,2,3072]{2,1,0:T(2,128)(2,1)S(1)}, u32[]{:S(2)}, u32[]{:S(2)}) async-start(bf16[64,2,3072]{2,1,0:T(2,128)(2,1)} %broadcast_select_fusion), calls=%async_computation.7 | async-start | bytes 1572864 | tf_op jit(solution)/shard_map/all_to_all | solution.py:37
  280.6 13.2 %fusion.4 = f32[64,2,16,768]{3,0,2,1:T(8,128)} fusion(bf16[64,2,16,1024]{3,2,1,0:T(8,128)(2,1)} %all-to-all-done.4, bf16[2,1024,768]{2,1,0:T(8,128)(2,1)} %all-gather.5.cloned.1.call-done), kind=kOutput, calls=%fused_computation.14 | convolution fusion | flops 3221225472 | bytes 13631488 | tf_op jit(solution)/shard_map/njcd,jdh->njch/dot_general | solution.py:65
  293.8 5.7 %convert_bitcast_fusion = bf16[64,2,16,1024]{3,0,2,1:T(8,128)(2,1)S(1)} fusion(f32[64,2,16,768]{3,0,2,1:T(8,128)} %fusion.4, bf16[2,384,1024]{2,1,0:T(8,128)(2,1)} %all-gather.3.cloned.1.call-done), kind=kOutput, calls=%fused_computation.10 | convolution fusion | flops 1617428480 | bytes 12058624 | tf_op jit(solution)/shard_map/njch,jhd->njcd/dot_general | solution.py:72
  299.5 4.5 %copy.62 = bf16[64,2,16,1024]{3,2,1,0:T(8,128)(2,1)} copy(bf16[64,2,16,1024]{3,0,2,1:T(8,128)(2,1)S(1)} %convert_bitcast_fusion) | data formatting | bytes 8388608 | tf_op jit(solution)/shard_map/convert_element_type | solution.py:74
  304.0 10.6 %all-to-all-start.5 = ((bf16[64,2,16,1024]{3,2,1,0:T(8,128)(2,1)}), bf16[64,2,16,1024]{3,2,1,0:T(8,128)(2,1)}, u32[]{:S(2)}, u32[]{:S(2)}) async-start(bf16[64,2,16,1024]{3,2,1,0:T(8,128)(2,1)} %copy.62), calls=%async_computation.5 | async-start | bytes 8388608 | tf_op jit(solution)/shard_map/all_to_all | solution.py:75
  314.7 0.1 add.114
  314.8 0.1 copy.53
  315.0 1.0 reshape.220
  316.0 0.1 copy.64
  316.1 1.3 reshape.219
  317.5 93.0 %all-to-all-done.5 = bf16[64,2,16,1024]{3,2,1,0:T(8,128)(2,1)} async-done(((bf16[64,2,16,1024]{3,2,1,0:T(8,128)(2,1)}), bf16[64,2,16,1024]{3,2,1,0:T(8,128)(2,1)}, u32[]{:S(2)}, u32[]{:S(2)}) %all-to-all-start.5) | async-done | bytes 4194336 | tf_op jit(solution)/shard_map/all_to_all | solution.py:75
  410.5 7.7 %gather_fusion.1 = bf16[1024,1024]{1,0:T(8,128)(2,1)S(1)} fusion(bf16[2048,1024]{1,0:T(8,128)(2,1)} %bitcast.20, s32[1024]{0:T(1024)S(1)} %broadcast_clamp_fusion), kind=kCustom, calls=%fused_computation.4 | custom fusion | bytes 4198400 | tf_op jit(solution)/shard_map/jit(_take)/gather | solution.py:77
  418.2 2.2 multiply_reduce_fusion
  (47 shorter events, 0.6 us)
Async XLA Ops:
  7.2 134.4 %copy-start = (bf16[128,1024]{1,0:T(8,128)(2,1)S(1)}, bf16[128,1024]{1,0:T(8,128)(2,1)}, u32[]{:S(2)}) copy-start(bf16[128,1024]{1,0:T(8,128)(2,1)} %param.11) | copy-start | bytes 786436
  7.2 33.5 %copy-start.4 = (bf16[2,2,48,1024]{3,2,1,0:T(8,128)(2,1)S(1)}, bf16[2,2,48,1024]{3,2,1,0:T(8,128)(2,1)}, u32[]{:S(2)}) copy-start(bf16[2,2,48,1024]{3,2,1,0:T(8,128)(2,1)} %param.15) | copy-start | bytes 1179652
  7.2 34.9 %copy-start.7 = (s32[128]{0:T(128)S(1)}, s32[128]{0:T(128)}, u32[]{:S(2)}) copy-start(s32[128]{0:T(128)} %param.18) | copy-start | bytes 1540
  7.2 34.9 %copy-start.8 = (s32[128]{0:T(128)S(1)}, s32[128]{0:T(128)}, u32[]{:S(2)}) copy-start(s32[128]{0:T(128)} %param.19) | copy-start | bytes 1540
  9.2 25.8 %all-to-all-start = ((bf16[2,64,768]{2,0,1:T(2,128)(2,1)}), bf16[2,64,768]{2,0,1:T(2,128)(2,1)S(1)}, u32[]{:S(2)}, u32[]{:S(2)}) async-start(bf16[2,64,768]{2,0,1:T(2,128)(2,1)} %copy.57), calls=%async_computation | async-start | bytes 393216 | tf_op jit(solution)/shard_map/all_to_all | solution.py:29
  35.0 20.2 %all-to-all-start.2 = ((bf16[2,64,1536]{2,0,1:T(2,128)(2,1)}), bf16[2,64,1536]{2,0,1:T(2,128)(2,1)S(1)}, u32[]{:S(2)}, u32[]{:S(2)}) async-start(bf16[2,64,1536]{2,0,1:T(2,128)(2,1)} %copy.59), calls=%async_computation.2 | async-start | bytes 786432 | tf_op jit(solution)/shard_map/all_to_all | solution.py:28
  55.2 20.8 %all-to-all-start.8 = ((bf16[2,64,1536]{2,0,1:T(2,128)(2,1)}), bf16[2,64,1536]{2,0,1:T(2,128)(2,1)S(1)}, u32[]{:S(2)}, u32[]{:S(2)}) async-start(bf16[2,64,1536]{2,0,1:T(2,128)(2,1)} %copy.65), calls=%async_computation.8 | async-start | bytes 786432 | tf_op jit(solution)/shard_map/all_to_all | solution.py:31
  76.0 17.2 %all-to-all-start.1 = ((bf16[64,2,768]{2,1,0:T(2,128)(2,1)}), bf16[64,2,768]{2,1,0:T(2,128)(2,1)S(1)}, u32[]{:S(2)}, u32[]{:S(2)}) async-start(bf16[64,2,768]{2,1,0:T(2,128)(2,1)} %broadcast_select_fusion.3), calls=%async_computation.1 | async-start | bytes 393216 | tf_op jit(solution)/shard_map/all_to_all | solution.py:36
  84.2 35.5 %copy-start.6 = (s32[128,8]{0,1:T(8,128)S(1)}, s32[128,8]{0,1:T(8,128)}, u32[]{:S(2)}) copy-start(s32[128,8]{0,1:T(8,128)} %param.16) | copy-start | bytes 12292
  84.2 36.0 %copy-start.1 = (bf16[2,2,128,768]{3,2,1,0:T(8,128)(2,1)S(1)}, bf16[2,2,128,768]{3,2,1,0:T(8,128)(2,1)}, u32[]{:S(2)}) copy-start(bf16[2,2,128,768]{3,2,1,0:T(8,128)(2,1)} %param.14) | copy-start | bytes 2359300
  93.2 20.2 %copy-start.2 = (bf16[64,2,768]{2,1,0:T(2,128)(2,1)}, bf16[64,2,768]{2,1,0:T(2,128)(2,1)S(1)}, u32[]{:S(2)}) copy-start(bf16[64,2,768]{2,1,0:T(2,128)(2,1)S(1)} %all-to-all-done.1) | copy-start | bytes 589828
  93.2 20.2 %all-to-all-start.3 = ((bf16[64,2,1536]{2,1,0:T(2,128)(2,1)}), bf16[64,2,1536]{2,1,0:T(2,128)(2,1)S(1)}, u32[]{:S(2)}, u32[]{:S(2)}) async-start(bf16[64,2,1536]{2,1,0:T(2,128)(2,1)} %all_to_all.116), calls=%async_computation.3 | async-start | bytes 786432 | tf_op jit(solution)/shard_map/all_to_all | solution.py:35
  113.5 20.8 %all-to-all-start.9 = ((bf16[64,2,1536]{2,1,0:T(2,128)(2,1)}), bf16[64,2,1536]{2,1,0:T(2,128)(2,1)S(1)}, u32[]{:S(2)}, u32[]{:S(2)}) async-start(bf16[64,2,1536]{2,1,0:T(2,128)(2,1)} %all_to_all.131), calls=%async_computation.9 | async-start | bytes 786432 | tf_op jit(solution)/shard_map/all_to_all | solution.py:38
  134.3 29.4 %all-to-all-start.6 = ((bf16[2,64,3072]{2,0,1:T(2,128)(2,1)}), bf16[2,64,3072]{2,0,1:T(2,128)(2,1)S(1)}, u32[]{:S(2)}, u32[]{:S(2)}) async-start(bf16[2,64,3072]{2,0,1:T(2,128)(2,1)} %copy.63), calls=%async_computation.6 | async-start | bytes 1572864 | tf_op jit(solution)/shard_map/all_to_all | solution.py:30
  163.7 7.6 %copy-start.3 = (bf16[64,2,768]{2,1,0:T(2,128)(2,1)S(1)}, bf16[64,2,768]{2,1,0:T(2,128)(2,1)}, u32[]{:S(2)}) copy-start(bf16[64,2,768]{2,1,0:T(2,128)(2,1)} %copy-done.2) | copy-start | bytes 589828
  163.7 102.4 %all-to-all-start.4 = ((bf16[64,2,16,1024]{3,2,1,0:T(8,128)(2,1)}), bf16[64,2,16,1024]{3,2,1,0:T(8,128)(2,1)}, u32[]{:S(2)}, u32[]{:S(2)}) async-start(bf16[64,2,16,1024]{3,2,1,0:T(8,128)(2,1)} %bitcast.50), calls=%async_computation.4 | async-start | bytes 8388608 | tf_op jit(solution)/shard_map/all_to_all | solution.py:67
  170.2 110.4 %all-gather.5.cloned.1.call-start = ((), (), s32[]{:S(2)}) async-start(), calls=%async_computation.11 | async-start | bytes 3538944 | tf_op jit(solution)/shard_map/all_gather | solution.py:45
  171.2 122.6 %all-gather.3.cloned.1.call-start = ((), (), s32[]{:S(2)}) async-start(), calls=%async_computation.10 | async-start | bytes 1769472 | tf_op jit(solution)/shard_map/all_gather | solution.py:46
  266.1 37.9 %all-to-all-start.7 = ((bf16[64,2,3072]{2,1,0:T(2,128)(2,1)}), bf16[64,2,3072]{2,1,0:T(2,128)(2,1)S(1)}, u32[]{:S(2)}, u32[]{:S(2)}) async-start(bf16[64,2,3072]{2,1,0:T(2,128)(2,1)} %broadcast_select_fusion), calls=%async_computation.7 | async-start | bytes 1572864 | tf_op jit(solution)/shard_map/all_to_all | solution.py:37
  304.0 10.8 %copy-start.5 = (f32[128,8]{0,1:T(8,128)S(1)}, f32[128,8]{0,1:T(8,128)}, u32[]{:S(2)}) copy-start(f32[128,8]{0,1:T(8,128)} %param.17) | copy-start | bytes 12292
  304.0 106.5 %all-to-all-start.5 = ((bf16[64,2,16,1024]{3,2,1,0:T(8,128)(2,1)}), bf16[64,2,16,1024]{3,2,1,0:T(8,128)(2,1)}, u32[]{:S(2)}, u32[]{:S(2)}) async-start(bf16[64,2,16,1024]{3,2,1,0:T(8,128)(2,1)} %copy.62), calls=%async_computation.5 | async-start | bytes 8388608 | tf_op jit(solution)/shard_map/all_to_all | solution.py:75
Sparse Core Ops, SparseCore 0:
  173.7 47.5 all-gather.4
  223.9 37.7 all-gather.2
where the time goes:
time: 433 us; the launch traced here: 428 us
  waiting for transfers between devices  258 us (60%)
  starting transfers between devices  83.1 us (19%)
  local copies, waits for them, and re-layouts  47 us (11%)
  matrix products  18.9 us (4%)
  between operations  14.7 us (3%)
  other arithmetic  6.19 us (1%)
    all_to_all x1, waiting for transfers between devices, on_device(): lax.all_to_all(result, 'exp', split_axis=0, concat_axis=0, tiled=True)  93 us
    all_to_all x1, waiting for transfers between devices, on_device(): lax.all_to_all(outgoing, 'exp', split_axis=0, concat_axis=0, tiled=True)  90.5 us
    scatter x1, local copies, waits for them, and re-layouts, on_device(): jnp.zeros((slot_count * capacity, width), jnp.bfloat16).at[target]  15.3 us
    all_to_all x1, starting transfers between devices, on_device(): lax.all_to_all(flat_out, 'exp', split_axis=1, concat_axis=0, tiled=True)  14.8 us
    all_to_all x1, starting transfers between devices, on_device(): lax.all_to_all(picked[2], 'exp', split_axis=0, concat_axis=1, tiled=True)  14.5 us
    all_to_all x1, waiting for transfers between devices, on_device(): lax.all_to_all(picked[0], 'exp', split_axis=0, concat_axis=1, tiled=True)  13.7 us
    dot_general x1, matrix products, on_device(): jnp.einsum('njcd,jdh->njch', lax.all_to_all(outgoing, 'exp', split_axis=0...  13.2 us
    all_to_all x1, waiting for transfers between devices, on_device(): lax.all_to_all(flat_in, 'exp', split_axis=1, concat_axis=0, tiled=True)  12.8 us
  transfers between devices with their start and end apart: 12, of which 9 were waited for; matrix products, arithmetic and copies ran while one was open for 13% of the time, Pallas kernels for 0%

commit v1 on v0

v1 whole, which is shorter than its diff:
```python
import functools
import heapq

import jax
import jax.numpy as jnp
from jax import lax
from jax.experimental import pallas as pl
from jax.experimental.pallas import tpu as pltpu
from jax.sharding import PartitionSpec as P

TOP = 8
TOK = 128
D = 1024
H = 384
NX, NZ, NY = 4, 8, 8
META = 8
ROWS = TOK + META
CAP = 16
CHIPS = NX * NZ
MESH = pl.DeviceIdType.MESH
VMEM_LIMIT = 62 * 1024 * 1024
TILES = 432
CHUNK = 7


def order_of(items):
    free, heap, started, arrived, ops = {}, [], set(), set(), []

    def start_ready(now):
        for name, (link, size, deps) in items.items():
            if name not in started and all(d in arrived for d in deps):
                begin = max(now, free.get(link, 0.0))
                free[link] = begin + size
                heapq.heappush(heap, (free[link] + (600.0 if link[0] != "c" else 100.0), len(started), name))
                started.add(name)
                ops.append(("start", name))

    start_ready(0.0)
    while heap:
        now, _, name = heapq.heappop(heap)
        arrived.add(name)
        ops.append(("wait", name))
        start_ready(now)
    return ops


def split(lo, hi, s):
    mid = lo + ((hi - lo) // 2 + 7) // 8 * 8
    return (lo, mid) if s > 0 else (mid, hi)


def place():
    y = lax.axis_index("grp")
    e = lax.axis_index("exp")
    c = lax.rem(e, 2)
    r = e // 2
    return y, e, c, r // NZ, lax.rem(r, NZ)


def chip_at(x, z, dx, dz):
    return lax.rem(x + dx + NX, NX) * NZ + lax.rem(z + dz + NZ, NZ)


def neighbour(link):
    y, e, c, x, z = place()
    axis, s = link
    if axis == "x":
        return (y, 2 * chip_at(x, z, s, 0) + c)
    if axis == "z":
        return (y, 2 * chip_at(x, z, 0, s) + c)
    if axis == "y":
        return (lax.rem(y + s + NY, NY), e)
    return (y, e + 1 - 2 * c)


def greet(links):
    barrier = pltpu.get_barrier_semaphore()
    for link in links:
        pl.semaphore_signal(barrier, inc=1, device_id=neighbour(link), device_id_type=MESH)
    pl.semaphore_wait(barrier, len(links))


TORUS = (("x", 1), ("x", -1), ("z", 1), ("z", -1))


def gather_items(pr):
    row, items = D * 2 / 46.5, {}

    def rows_of(name):
        lo, hi = (0, pr) if name[0][0] == "P" else (pr, ROWS)
        half = name[-1] == (4 if name[0][1] == "Z" else 2)
        return split(lo, hi, name[-2]) if half else (lo, hi)

    def add(name, link, deps):
        lo, hi = rows_of(name)
        items[name] = (link, (hi - lo) * row, deps)

    for s in (1, -1):
        for d in (1, 2, 3, 4):
            add(("PZ", s, d), ("z", s), [("PZ", s, d - 1)] if d > 1 else [])
        for d in (1, 2):
            add(("QX", s, d), ("x", s), [("QX", s, d - 1)] if d > 1 else [])
    for s in (1, -1):
        for d in (1, 2, 3, 4):
            dep = lambda k: [(k, s, d - 1)] if d > 1 else []
            part = 0.5 if d == 4 else 1.0
            items[("WI", s, d)] = (("y", s), part * 2 * 128 * 768 * 2 / 46.5, dep("WI"))
            items[("WO", s, d)] = (("y", s), part * 2 * 48 * 1024 * 2 / 46.5, dep("WO"))
    for dz in (0, 1, 7, 2, 6, 3, 5, 4):
        for s in (1, -1):
            for d in (1, 2):
                if d == 2:
                    deps = [("PX", dz, s, 1)]
                elif dz == 0:
                    deps = []
                elif dz == 4:
                    deps = [("PZ", 1, 4), ("PZ", -1, 4)]
                else:
                    deps = [("PZ", -1, dz)] if dz < 4 else [("PZ", 1, 8 - dz)]
                add(("PX", dz, s, d), ("x", s), deps)
    for dx in (0, 1, 3, 2):
        for s in (1, -1):
            for d in (1, 2, 3, 4):
                if d > 1:
                    deps = [("QZ", dx, s, d - 1)]
                elif dx == 0:
                    deps = []
                elif dx == 2:
                    deps = [("QX", 1, 2), ("QX", -1, 2)]
                else:
                    deps = [("QX", -1, 1)] if dx == 1 else [("QX", 1, 1)]
                add(("QZ", dx, s, d), ("z", s), deps)
    for dy in range(NY):
        for k, size in (("WI", 393216), ("WO", 196608)):
            if dy == 0:
                deps = []
            elif dy == 4:
                deps = [(k, 1, 4), (k, -1, 4)]
            else:
                deps = [(k, -1, dy)] if dy < 4 else [(k, 1, 8 - dy)]
            items[("S" + k, dy)] = (("c", 0), size / 300.0, deps)
    return items, rows_of


def gather_kernel(pr, xt, wi, wo, g, gi, go, ssem, rsem, lsem):
    y, e, c, x, z = place()
    items, rows_of = gather_items(pr)
    index = {name: i for i, name in enumerate(items)}
    greet(TORUS + (("y", 1), ("y", -1), ("c", 0)))
    own = chip_at(x, z, 0, 0)
    span_i, span_o = wi.shape[1], wo.shape[1]

    def weights(k, dy, slots, core):
        ref, span = (gi, span_i) if k == "WI" else (go, span_o)
        at = pl.multiple_of(lax.rem(y + dy + NY, NY) * span, span)
        return ref.at[pl.ds(2 * core + slots[0], slots[1]), pl.ds(at, span)]

    def ends(name, shift):
        kind = name[0]
        if kind[0] == "S":
            k, dy = kind[1:], name[1]
            core = c if shift else 1 - c
            dst = weights(k, dy, (0, 2), core)
            return ((wi if k == "WI" else wo) if dy == 0 else dst), dst
        if kind[0] == "W":
            s, d = name[1:]
            slots = (0, 2) if d < 4 else ((0, 1) if s > 0 else (1, 1))
            dst = weights(kind, -s * (d - shift), slots, c)
            return ((wi if kind == "WI" else wo) if d == 1 else dst), dst
        lo, hi = rows_of(name)
        s, d = name[-2:]
        off = -s * (d - shift)
        if kind == "PZ":
            dx, dz = 0, off
        elif kind == "QX":
            dx, dz = off, 0
        elif kind == "PX":
            dx, dz = off, name[1]
        else:
            dx, dz = name[1], off
        dst = g.at[chip_at(x, z, dx, dz), pl.ds(lo, hi - lo)]
        mine = shift == 1 and dx % NX == 0 and dz % NZ == 0
        return (xt.at[pl.ds(lo, hi - lo)] if mine else dst), dst

    def copy(name, shift):
        src, dst = ends(name, shift)
        i = index[name]
        return pltpu.make_async_remote_copy(
            src_ref=src if shift else dst,
            dst_ref=dst,
            send_sem=ssem.at[i],
            recv_sem=rsem.at[i],
            device_id=neighbour(items[name][0]),
            device_id_type=MESH,
        )

    local = [
        pltpu.make_async_copy(xt, g.at[own], lsem.at[0]),
        pltpu.make_async_copy(wi, weights("WI", 0, (0, 2), c), lsem.at[1]),
        pltpu.make_async_copy(wo, weights("WO", 0, (0, 2), c), lsem.at[2]),
    ]
    for name_op in order_of(items):
        op, name = name_op
        if op == "start":
            copy(name, 1).start()
        else:
            copy(name, 0).wait_recv()
        if local and op == "wait":
            for item in local:
                item.start()
            done, local = local, []
    for item in done:
        item.wait()
    for name in items:
        copy(name, 1).wait_send()


def gather(pr, xt, wi, wo):
    count = len(gather_items(pr)[0])
    any_space = pl.BlockSpec(memory_space=pl.ANY)
    vmem = pl.BlockSpec(memory_space=pltpu.VMEM)
    return pl.pallas_call(
        functools.partial(gather_kernel, pr),
        out_shape=(
            jax.ShapeDtypeStruct((CHIPS, ROWS, D), jnp.bfloat16),
            jax.ShapeDtypeStruct((4, D, 2 * H), jnp.bfloat16),
            jax.ShapeDtypeStruct((4, H, D), jnp.bfloat16),
        ),
        in_specs=[vmem] * 3,
        out_specs=(any_space,) * 3,
        scratch_shapes=[
            pltpu.SemaphoreType.DMA((count,)),
            pltpu.SemaphoreType.DMA((count,)),
            pltpu.SemaphoreType.DMA((3,)),
        ],
        compiler_params=pltpu.CompilerParams(
            collective_id=0, has_side_effects=True, vmem_limit_bytes=VMEM_LIMIT
        ),
        cost_estimate=pl.CostEstimate(flops=0, bytes_accessed=200_000_000, transcendentals=0),
        name="gather",
    )(xt, wi, wo)


STEP = 8


def expert_kernel(es, g, wi, wo, part, gv, wiv, wov, xs, ys, cnt, wgt, rank, sel, outv, isem, wsem, osem):
    nchunk = CHIPS // STEP
    for n in range(nchunk):
        pltpu.make_async_copy(g.at[pl.ds(n * STEP, STEP)], gv.at[pl.ds(n * STEP, STEP)], isem.at[n]).start()
    for j in range(4):
        pltpu.make_async_copy(wi.at[j], wiv.at[j], wsem.at[j]).start()
        pltpu.make_async_copy(wo.at[j], wov.at[j], wsem.at[4 + j]).start()
    tri = (
        lax.broadcasted_iota(jnp.int32, (TOK, TOK), 0) <= lax.broadcasted_iota(jnp.int32, (TOK, TOK), 1)
    ).astype(jnp.bfloat16)
    line = lax.broadcasted_iota(jnp.int32, (CAP, TOK), 0).astype(jnp.float32)
    experts = [es[j].astype(jnp.float32) for j in range(4)]
    for n in range(nchunk):
        pltpu.make_async_copy(
            g.at[pl.ds(n * STEP, STEP)], gv.at[pl.ds(n * STEP, STEP)], isem.at[n]
        ).wait()

        def count(i, _):
            b = n * STEP + i
            meta = gv[b, TOK:ROWS, 0:256].astype(jnp.float32)
            ids, share = meta[:, 0:TOK], meta[:, TOK:256]
            named = [ids == experts[j] for j in range(4)]
            ones = [jnp.sum(jnp.where(m, 1.0, 0.0), axis=0, keepdims=True) for m in named]
            held = [jnp.sum(jnp.where(m, share, 0.0), axis=0, keepdims=True) for m in named]
            rows = pl.ds(pl.multiple_of(b * 8, 8), 8)
            cnt[rows, :] = jnp.concatenate(ones + ones, axis=0)
            wgt[rows, :] = jnp.concatenate(held + held, axis=0)
            return 0

        lax.fori_loop(0, STEP, count, 0)
        rows = pl.ds(n * STEP * 8, STEP * 8)
        chosen = cnt[rows, :]
        upto = jnp.dot(chosen.astype(jnp.bfloat16), tri, preferred_element_type=jnp.float32)
        rank[rows, :] = jnp.where(chosen > 0.5, upto - 1.0, -1.0)

        def pick(i, _):
            b = n * STEP + i
            rows = pl.ds(pl.multiple_of(b * 8, 8), 8)
            place8, held8 = rank[rows, :], wgt[rows, :]
            hit = [line == place8[j : j + 1, :] for j in range(4)]
            onehot = jnp.concatenate([jnp.where(m, 1.0, 0.0) for m in hit], axis=0)
            weight = jnp.concatenate(
                [jnp.where(hit[j], held8[j : j + 1, :], 0.0) for j in range(4)], axis=0
            )
            sel[b] = weight.astype(jnp.bfloat16)
            got = jnp.dot(
                onehot.astype(jnp.bfloat16), gv[b, 0:TOK, :], preferred_element_type=jnp.float32
            ).astype(jnp.bfloat16)
            at = pl.ds(pl.multiple_of(b * CAP, CAP), CAP)
            for j in range(4):
                xs[j, at, :] = got[j * CAP : (j + 1) * CAP, :]
            return 0

        lax.fori_loop(0, STEP, pick, 0, unroll=2)
    for j in range(4):
        pltpu.make_async_copy(wi.at[j], wiv.at[j], wsem.at[j]).wait()
        pltpu.make_async_copy(wo.at[j], wov.at[j], wsem.at[4 + j]).wait()

    def mlp(i, _):
        j, at = i // 2, pl.ds(pl.multiple_of(lax.rem(i, 2) * 256, 256), 256)
        both = jnp.dot(xs[j, at, :], wiv[j], preferred_element_type=jnp.float32)
        hidden = (jax.nn.silu(both[:, :H]) * both[:, H:]).astype(jnp.bfloat16)
        ys[j, at, :] = jnp.dot(hidden, wov[j], preferred_element_type=jnp.float32).astype(jnp.bfloat16)
        return 0

    lax.fori_loop(0, 8, mlp, 0)
    for n in range(nchunk):

        def spread(i, _):
            b = n * STEP + i
            at = pl.ds(pl.multiple_of(b * CAP, CAP), CAP)
            rows = jnp.concatenate([ys[j, at, :] for j in range(4)], axis=0)
            outv[b] = lax.dot_general(
                sel[b], rows, (((0,), (0,)), ((), ())), preferred_element_type=jnp.float32
            ).astype(jnp.bfloat16)
            return 0

        lax.fori_loop(0, STEP, spread, 0, unroll=2)
        pltpu.make_async_copy(outv.at[pl.ds(n * STEP, STEP)], part.at[pl.ds(n * STEP, STEP)], osem.at[n]).start()
    for n in range(nchunk):
        pltpu.make_async_copy(
            outv.at[pl.ds(n * STEP, STEP)], part.at[pl.ds(n * STEP, STEP)], osem.at[n]
        ).wait()


def experts_of(es, g, wi, wo):
    any_space = pl.BlockSpec(memory_space=pl.ANY)
    nchunk = CHIPS // STEP
    return pl.pallas_call(
        expert_kernel,
        out_shape=jax.ShapeDtypeStruct((CHIPS, TOK, D), jnp.bfloat16),
        in_specs=[pl.BlockSpec(memory_space=pltpu.SMEM)] + [any_space] * 3,
        out_specs=any_space,
        scratch_shapes=[
            pltpu.VMEM((CHIPS, ROWS, D), jnp.bfloat16),
            pltpu.VMEM((4, D, 2 * H), jnp.bfloat16),
            pltpu.VMEM((4, H, D), jnp.bfloat16),
            pltpu.VMEM((4, CHIPS * CAP, D), jnp.bfloat16),
            pltpu.VMEM((4, CHIPS * CAP, D), jnp.bfloat16),
            pltpu.VMEM((CHIPS * 8, TOK), jnp.float32),
            pltpu.VMEM((CHIPS * 8, TOK), jnp.float32),
            pltpu.VMEM((CHIPS * 8, TOK), jnp.float32),
            pltpu.VMEM((CHIPS, 4 * CAP, TOK), jnp.bfloat16),
            pltpu.VMEM((CHIPS, TOK, D), jnp.bfloat16),
            pltpu.SemaphoreType.DMA((nchunk,)),
            pltpu.SemaphoreType.DMA((8,)),
            pltpu.SemaphoreType.DMA((nchunk,)),
        ],
        compiler_params=pltpu.CompilerParams(vmem_limit_bytes=VMEM_LIMIT),
        cost_estimate=pl.CostEstimate(flops=6_000_000_000, bytes_accessed=40_000_000, transcendentals=0),
        name="experts",
    )(es, g, wi, wo)


def reduce_items(pr):
    row, items, span = D * 2 / 46.5, {}, {}

    def add(name, link, deps, lo, hi):
        span[name] = (lo, hi)
        items[name] = (link, (hi - lo) * row, deps)

    for dz in (4, 3, 5, 2, 6, 1, 7, 0):
        for s in (1, -1):
            add(("A", dz, s), ("x", s), [], *split(0, pr, s))
    for dx in (2, 1, 3, 0):
        for s in (1, -1):
            add(("D", dx, s, 4), ("z", s), [], *split(pr, TOK, s))
    for dz in (4, 3, 5, 2, 6, 1, 7, 0):
        for s in (1, -1):
            add(("B", dz, s), ("x", s), [("A", dz, s)], 0, pr)
    for s in (1, -1):
        for d in (4, 3, 2, 1):
            dz = (s * d) % NZ
            deps = [("B", dz, 1), ("B", dz, -1)] + ([("C", s, d + 1)] if d < 4 else [])
            add(("C", s, d), ("z", s), deps, *(split(0, pr, s) if d == 4 else (0, pr)))
    for dx in (2, 1, 3, 0):
        for s in (1, -1):
            for d in (3, 2, 1):
                add(("D", dx, s, d), ("z", s), [("D", dx, s, d + 1)], pr, TOK)
    for s in (1, -1):
        for d in (2, 1):
            dx = (s * d) % NX
            deps = [("D", dx, 1, 1), ("D", dx, -1, 1)] + ([("E", s, 2)] if d < 2 else [])
            add(("E", s, d), ("x", s), deps, *(split(pr, TOK, s) if d == 2 else (pr, TOK)))
    return items, span


def reduce_kernel(pr, part, out, pv, land, ssem, rsem, lsem):
    y, e, c, x, z = place()
    items, span = reduce_items(pr)
    index, base, top = {}, {}, 0
    for i, name in enumerate(items):
        index[name], base[name] = i, top
        top += span[name][1] - span[name][0]
    for b in range(CHIPS // 4):
        pltpu.make_async_copy(part.at[pl.ds(4 * b, 4)], pv.at[pl.ds(4 * b, 4)], lsem.at[b]).start()
    greet(TORUS)
    for b in range(CHIPS // 4):
        pltpu.make_async_copy(part.at[pl.ds(4 * b, 4)], pv.at[pl.ds(4 * b, 4)], lsem.at[b]).wait()

    def block(name, shift):
        kind, s = name[0], name[2] if name[0] in "ABD" else name[1]
        if kind == "A":
            return chip_at(x, z, s * (2 - shift), name[1])
        if kind == "B":
            return chip_at(x, z, s * (1 - shift), name[1])
        d = name[-1] - shift
        if kind == "C":
            return chip_at(x, z, 0, s * d)
        if kind == "D":
            return chip_at(x, z, name[1], s * d)
        return chip_at(x, z, s * d, 0)

    def copy(name):
        lo, hi = span[name]
        i = index[name]
        return pltpu.make_async_remote_copy(
            src_ref=pv.at[block(name, 0), pl.ds(lo, hi - lo)],
            dst_ref=land.at[pl.ds(base[name], hi - lo)],
            send_sem=ssem.at[i],
            recv_sem=rsem.at[i],
            device_id=neighbour(items[name][0]),
            device_id_type=MESH,
        )

    def fold(name):
        lo, hi = span[name]
        b = block(name, 1)

        def body(i, _):
            to = pl.ds(pl.multiple_of(lo + i * 16, 16), 16)
            src = pl.ds(pl.multiple_of(base[name] + i * 16, 16), 16)
            pv[b, to, :] = (
                pv[b, to, :].astype(jnp.float32) + land[src, :].astype(jnp.float32)
            ).astype(jnp.bfloat16)
            return 0

        lax.fori_loop(0, (hi - lo) // 16, body, 0)

    for op, name in order_of(items):
        if op == "start":
            copy(name).start()
        else:
            copy(name).wait_recv()
            fold(name)
    out[...] = pv[chip_at(x, z, 0, 0)]
    for name in items:
        copy(name).wait_send()


def reduce(pr, part):
    items, span = reduce_items(pr)
    count, rows = len(items), sum(hi - lo for lo, hi in span.values())
    return pl.pallas_call(
        functools.partial(reduce_kernel, pr),
        out_shape=jax.ShapeDtypeStruct((TOK, D), jnp.bfloat16),
        in_specs=[pl.BlockSpec(memory_space=pl.ANY)],
        out_specs=pl.BlockSpec(memory_space=pltpu.VMEM),
        scratch_shapes=[
            pltpu.VMEM((CHIPS, TOK, D), jnp.bfloat16),
            pltpu.VMEM((rows, D), jnp.bfloat16),
            pltpu.SemaphoreType.DMA((count,)),
            pltpu.SemaphoreType.DMA((count,)),
            pltpu.SemaphoreType.DMA((CHIPS // 4,)),
        ],
        compiler_params=pltpu.CompilerParams(
            collective_id=1, has_side_effects=True, vmem_limit_bytes=VMEM_LIMIT
        ),
        cost_estimate=pl.CostEstimate(flops=0, bytes_accessed=200_000_000, transcendentals=0),
        name="reduce",
    )(part)


def tiles_of(array):
    slots, columns = array.shape[0], array.shape[-1]
    rows = array.size // slots // columns
    tiled = array.reshape(slots, rows // 8, 8, columns // 128, 128)
    return tiled.transpose(0, 1, 3, 2, 4).reshape(slots, -1, 8, 128)


def untile(tiles, shape):
    slots, columns = shape[0], shape[-1]
    tiled = tiles.reshape(slots, -1, columns // 128, 8, 128)
    return tiled.transpose(0, 1, 3, 2, 4).reshape(shape)


def on_device(
    tokens, w_in, w_out, moments_in, moments_out, expert_ids, route_weights, old_plan, new_plan
):
    devices = lax.axis_size("exp")
    slots = 2 * devices
    slot_index = jnp.arange(slots, dtype=jnp.int32)
    same_expert = new_plan[:, None] == old_plan[None, :]
    source = jnp.min(jnp.where(same_expert, slot_index[None, :], slots), axis=1)

    state = [w_in, w_out, moments_in, moments_out]
    pooled = jnp.concatenate(
        [tiles_of(a) for a in state] + [jnp.zeros((2, 64 * CHUNK - TILES, 8, 128), jnp.bfloat16)], axis=1
    )
    pooled = pooled.reshape(2, devices, CHUNK * 8, 128).transpose(1, 0, 2, 3)
    spread = lax.all_to_all(pooled, "exp", split_axis=0, concat_axis=0, tiled=True)

    share = route_weights / jnp.sum(route_weights, axis=1, keepdims=True)
    meta = jnp.concatenate(
        [
            expert_ids.T.astype(jnp.bfloat16),
            share.T.astype(jnp.bfloat16),
            jnp.zeros((META, D - 2 * TOK), jnp.bfloat16),
        ],
        axis=1,
    )
    g, gi, go = gather(96, jnp.concatenate([tokens, meta], axis=0), w_in, w_out)

    picked = jnp.take(spread.reshape(slots, CHUNK * 8, 128), source, axis=0)
    landed = lax.all_to_all(
        picked.reshape(devices, 2, CHUNK * 8, 128), "exp", split_axis=0, concat_axis=0, tiled=True
    )

    earlier = (old_plan[:, None] == old_plan[None, :]) & (slot_index[None, :] < slot_index[:, None])
    computes = jnp.where(jnp.any(earlier, axis=1), -1, old_plan)
    es = lax.dynamic_slice(computes, (lax.axis_index("exp") // 2 * 4,), (4,))
    mixed = reduce(96, experts_of(es, g, gi, go))

    tiles = landed.transpose(1, 0, 2, 3).reshape(2, 64 * CHUNK, 8, 128)
    outs, at = [], 0
    for a in state:
        count = a.size // 2 // 1024
        outs.append(untile(tiles[:, at : at + count], a.shape))
        at += count
    return (mixed, *outs)


def solution(mesh):
    return jax.shard_map(
        on_device,
        mesh=mesh,
        in_specs=(
            P(("grp", "exp"), None),
            P("exp", "grp", None),
            P("exp", "grp", None),
            P("exp", None, "grp", None),
            P("exp", None, "grp", None),
            P(("grp", "exp"), None),
            P(("grp", "exp"), None),
            P(),
            P(),
        ),
        out_specs=(
            P(("grp", "exp"), None),
            P("exp", "grp", None),
            P("exp", "grp", None),
            P("exp", None, "grp", None),
            P("exp", None, "grp", None),
        ),
        check_vma=False,
    )
```

time: 433 us -> 265 us (0.61)
  waiting for transfers between devices: 258 us -> 45 us
  Pallas kernels: 0 us -> 181 us
  starting transfers between devices: 83.1 us -> 21.1 us
  local copies, waits for them, and re-layouts: 47 us -> 11 us
  matrix products: 18.9 us -> 0 us
  between operations: 14.7 us -> 0.87 us
    all_to_all x10 -> x2, waiting for transfers between devices: 258 us -> 45 us  [the longest x1 45 us: on_device(): lax.all_to_all(pooled, 'exp', split_axis=0, concat_axis=0, tiled=True)]
    pallas_call x0 -> x3, Pallas kernels: none -> 181 us  [the longest x1 97.2 us: gather(): pl.pallas_call(functools.partial(gather_kernel, pr), out_shape=(jax.Shape...]
    all_to_all x10 -> x2, starting transfers between devices: 83 us -> 21.1 us  [the longest x1 15 us: on_device(): lax.all_to_all(pooled, 'exp', split_axis=0, concat_axis=0, tiled=True)]
    dot_general x2 -> x0, matrix products: 18.9 us -> none  [the longest x1 13.2 us: on_device(): jnp.einsum('njcd,jdh->njch', lax.all_to_all(outgoing, 'exp', split_axis=0...]
    scatter x1 -> x0, local copies, waits for them, and re-layouts: 15.3 us -> none  [on_device(): jnp.zeros((slot_count * capacity, width), jnp.bfloat16).at[target]]
    all_to_all x18 -> x0, local copies, waits for them, and re-layouts: 10.6 us -> none  [the longest x3 2.45 us: on_device(): lax.all_to_all(flat_moments_in, 'exp', split_axis=1, concat_axis=0, tiled...]
    gather x7 -> x1, local copies, waits for them, and re-layouts: 11.8 us -> 2.07 us  [on_device(): picked = jnp.take(spread.reshape(slots, CHUNK * 8, 128), source, axis=0)]
    convert_element_type x1 -> x0, local copies, waits for them, and re-layouts: 4.5 us -> none  [on_device(): result = jnp.einsum('njch,jhd->njcd', hidden, full_out, preferred_element...]
  transfers between devices with their start and end apart: 12 -> 2, of which waited for: 9 -> 1; matrix products, arithmetic and copies ran while one was open for 13% -> 1% of each run, Pallas kernels for 0% -> 69%
where the time goes in v1:
time: 265 us; the launch traced here: 263 us
  Pallas kernels  181 us (68%)
  waiting for transfers between devices  45 us (17%)
  starting transfers between devices  21.1 us (8%)
  local copies, waits for them, and re-layouts  11 us (4%)
  other arithmetic  4.14 us (2%)
    pallas_call x1, Pallas kernels, gather(): pl.pallas_call(functools.partial(gather_kernel, pr), out_shape=(jax.Shape...  97.2 us
    pallas_call x1, Pallas kernels, reduce(): pl.pallas_call(functools.partial(reduce_kernel, pr), out_shape=jax.ShapeD...  58.9 us
    all_to_all x1, waiting for transfers between devices, on_device(): lax.all_to_all(pooled, 'exp', split_axis=0, concat_axis=0, tiled=True)  45 us
    pallas_call x1, Pallas kernels, experts_of(): pl.pallas_call(expert_kernel, out_shape=jax.ShapeDtypeStruct((CHIPS, TOK,...  24.5 us
    all_to_all x1, starting transfers between devices, on_device(): lax.all_to_all(pooled, 'exp', split_axis=0, concat_axis=0, tiled=True)  15 us
    all_to_all x1, starting transfers between devices, on_device(): lax.all_to_all(picked.reshape(devices, 2, CHUNK * 8, 128), 'exp', split_a...  6.14 us
  transfers between devices with their start and end apart: 2, of which 1 were waited for; matrix products, arithmetic and copies ran while one was open for 1% of the time, Pallas kernels for 69%

profile of v1, /device:TPU:1, one launch (start us, length us, event | category | flops | bytes accessed | tf_op | source)
XLA Modules:
  0.0 262.7 jit_solution(4592884531432170895)
XLA Ops:
  0.6 0.0 copy-start.1
  0.6 1.1 constant_dynamic-update-slice_fusion.3
  1.7 1.0 constant_dynamic-update-slice_fusion.2
  2.7 1.2 constant_dynamic-update-slice_fusion.1
  3.9 0.0 copy-done.1
  3.9 0.1 constant_dynamic-update-slice_fusion
  4.0 1.4 copy.19
  5.4 0.0 copy-start.5
  5.4 0.0 copy-start.6
  5.4 15.0 %all-to-all-start = ((bf16[64,2,56,128]{3,2,1,0:T(8,128)(2,1)}), bf16[64,2,56,128]{3,2,1,0:T(8,128)(2,1)S(1)}, u32[]{:S(2)}, u32[]{:S(2)}) async-start(bf16[64,2,56,128]{3,2,1,0:T(8,128)(2,1)} %copy.19), calls=%async_computation | async-start | bytes 3670016 | tf_op jit(solution)/shard_map/all_to_all | solution.py:507
  20.4 0.0 copy-done.5
  20.4 0.0 copy-done.6
  20.4 0.2 select_reduce_fusion
  20.6 0.1 reduce_min.14
  20.8 45.0 %all-to-all-done = bf16[64,2,56,128]{3,2,1,0:T(8,128)(2,1)S(1)} async-done(((bf16[64,2,56,128]{3,2,1,0:T(8,128)(2,1)}), bf16[64,2,56,128]{3,2,1,0:T(8,128)(2,1)S(1)}, u32[]{:S(2)}, u32[]{:S(2)}) %all-to-all-start) | async-done | bytes 1835040 | tf_op jit(solution)/shard_map/all_to_all | solution.py:507
  65.8 2.1 gather_fusion
  67.8 3.0 %broadcast_select_fusion = bf16[64,2,56,128]{3,2,1,0:T(8,128)(2,1)} fusion(bf16[64,2,56,128]{3,2,1,0:T(8,128)(2,1)} %bitcast.57, pred[64,2]{1,0:T(8,128)(4,1)S(1)} %compare_and_fusion), kind=kLoop, calls=%fused_computation.1 | loop fusion | flops 917504 | bytes 3670144 | tf_op jit(solution)/shard_map/jit(_take)/select_n | solution.py:520
  70.8 0.0 copy-start.3
  70.8 0.0 copy-start.4
  70.8 0.0 copy-start.2
  70.8 6.1 %all-to-all-start.1 = ((bf16[64,2,56,128]{3,2,1,0:T(8,128)(2,1)}), bf16[64,2,56,128]{3,2,1,0:T(8,128)(2,1)S(1)}, u32[]{:S(2)}, u32[]{:S(2)}) async-start(bf16[64,2,56,128]{3,2,1,0:T(8,128)(2,1)} %broadcast_select_fusion), calls=%async_computation.1 | async-start | bytes 3670016 | tf_op jit(solution)/shard_map/all_to_all | solution.py:521
  77.0 0.0 copy-done.3
  77.0 0.0 copy-done.4
  77.1 0.0 copy-done.2
  77.1 0.7 maximum_maximum_fusion.xt
  77.8 97.2 %gather.11 = (bf16[32,136,1024]{2,1,0:T(8,128)(2,1)}, bf16[4,1024,768]{2,1,0:T(8,128)(2,1)}, bf16[4,384,1024]{2,1,0:T(8,128)(2,1)}) custom-call(bf16[136,1024]{1,0:T(8,128)(2,1)} %maximum_maximum_fusion.xt, bf16[2,128,768]{2,1,0:T(8,128)(2,1)} %wi.1, bf16[2,48,1024]{2,1,0:T(8,128)(2,1)} %wo.1), custom_call_target="tpu_custom_call" | custom-call | bytes 200000000 | tf_op jit(solution)/shard_map/gather/pallas_call | solution.py:222
  175.1 0.2 fusion.1
  175.3 0.6 dynamic_slice.3.es
  175.8 24.5 %experts.1.part = bf16[32,128,1024]{2,1,0:T(8,128)(2,1)} custom-call(s32[4]{0:T(128)} %dynamic_slice.3.es, bf16[32,136,1024]{2,1,0:T(8,128)(2,1)} %get-tuple-element.8.g, bf16[4,1024,768]{2,1,0:T(8,128)(2,1)} %get-tuple-element.9.wi, bf16[4,384,1024]{2,1,0:T(8,128)(2,1)} %get-tuple-element.10.wo), custom_call_target="tpu_custom_call" | custom-call | flops 6000000000 | bytes 40000000 | tf_op jit(solution)/shard_map/experts/pallas_call | solution.py:335
  200.4 58.9 %reduce.1 = bf16[128,1024]{1,0:T(8,128)(2,1)} custom-call(bf16[32,128,1024]{2,1,0:T(8,128)(2,1)} %experts.1.part), custom_call_target="tpu_custom_call" | custom-call | bytes 200000000 | tf_op jit(solution)/shard_map/reduce/pallas_call | solution.py:460
  259.3 0.0 all-to-all-done.1
  259.3 0.1 copy.20
  259.5 0.0 copy-start
  259.5 0.9 fusion.4
  260.4 0.9 slice.20
  261.3 0.7 slice.19
  262.0 0.0 copy-done
  262.0 0.7 copy.26
  (9 shorter events, 0.1 us)
Async XLA Ops:
  0.6 3.3 %copy-start.1 = (bf16[2,2,48,1024]{3,2,1,0:T(8,128)(2,1)S(1)}, bf16[2,2,48,1024]{3,2,1,0:T(8,128)(2,1)}, u32[]{:S(2)}) copy-start(bf16[2,2,48,1024]{3,2,1,0:T(8,128)(2,1)} %param.13) | copy-start | bytes 1179652
  5.4 15.0 %copy-start.5 = (s32[128]{0:T(128)S(1)}, s32[128]{0:T(128)}, u32[]{:S(2)}) copy-start(s32[128]{0:T(128)} %param.17) | copy-start | bytes 1540
  5.4 15.0 %copy-start.6 = (s32[128]{0:T(128)S(1)}, s32[128]{0:T(128)}, u32[]{:S(2)}) copy-start(s32[128]{0:T(128)} %param.16) | copy-start | bytes 1540
  5.4 60.3 %all-to-all-start = ((bf16[64,2,56,128]{3,2,1,0:T(8,128)(2,1)}), bf16[64,2,56,128]{3,2,1,0:T(8,128)(2,1)S(1)}, u32[]{:S(2)}, u32[]{:S(2)}) async-start(bf16[64,2,56,128]{3,2,1,0:T(8,128)(2,1)} %copy.19), calls=%async_computation | async-start | bytes 3670016 | tf_op jit(solution)/shard_map/all_to_all | solution.py:507
  70.8 6.2 %copy-start.3 = (f32[128,8]{0,1:T(8,128)S(1)}, f32[128,8]{0,1:T(8,128)}, u32[]{:S(2)}) copy-start(f32[128,8]{0,1:T(8,128)} %param.15) | copy-start | bytes 12292
  70.8 6.2 %copy-start.4 = (s32[128,8]{0,1:T(8,128)S(1)}, s32[128,8]{0,1:T(8,128)}, u32[]{:S(2)}) copy-start(s32[128,8]{0,1:T(8,128)} %param.14) | copy-start | bytes 12292
  70.8 6.2 %copy-start.2 = (bf16[128,1024]{1,0:T(8,128)(2,1)S(1)}, bf16[128,1024]{1,0:T(8,128)(2,1)}, u32[]{:S(2)}) copy-start(bf16[128,1024]{1,0:T(8,128)(2,1)} %param.9) | copy-start | bytes 786436
  70.8 188.5 %all-to-all-start.1 = ((bf16[64,2,56,128]{3,2,1,0:T(8,128)(2,1)}), bf16[64,2,56,128]{3,2,1,0:T(8,128)(2,1)S(1)}, u32[]{:S(2)}, u32[]{:S(2)}) async-start(bf16[64,2,56,128]{3,2,1,0:T(8,128)(2,1)} %broadcast_select_fusion), calls=%async_computation.1 | async-start | bytes 3670016 | tf_op jit(solution)/shard_map/all_to_all | solution.py:521
  259.5 2.6 copy-start

commit v2 on v1

--- a/solution.py
+++ b/solution.py
@@ -21,6 +21,8 @@
 VMEM_LIMIT = 62 * 1024 * 1024
 TILES = 432
 CHUNK = 7
+GATHER_ROWS = 104
+REDUCE_ROWS = 96
 
 
 def order_of(items):
@@ -263,8 +265,8 @@
 
         def count(i, _):
             b = n * STEP + i
-            meta = gv[b, TOK:ROWS, 0:256].astype(jnp.float32)
-            ids, share = meta[:, 0:TOK], meta[:, TOK:256]
+            meta = gv[b, TOK:ROWS, 0 : 3 * TOK].astype(jnp.float32)
+            ids, share = meta[:, 0:TOK], meta[:, TOK : 2 * TOK] + meta[:, 2 * TOK :]
             named = [ids == experts[j] for j in range(4)]
             ones = [jnp.sum(jnp.where(m, 1.0, 0.0), axis=0, keepdims=True) for m in named]
             held = [jnp.sum(jnp.where(m, share, 0.0), axis=0, keepdims=True) for m in named]
@@ -288,7 +290,9 @@
             weight = jnp.concatenate(
                 [jnp.where(hit[j], held8[j : j + 1, :], 0.0) for j in range(4)], axis=0
             )
-            sel[b] = weight.astype(jnp.bfloat16)
+            high = weight.astype(jnp.bfloat16)
+            sel[b, 0 : 4 * CAP, :] = high
+            sel[b, 4 * CAP :, :] = (weight - high.astype(jnp.float32)).astype(jnp.bfloat16)
             got = jnp.dot(
                 onehot.astype(jnp.bfloat16), gv[b, 0:TOK, :], preferred_element_type=jnp.float32
             ).astype(jnp.bfloat16)
@@ -315,7 +319,7 @@
         def spread(i, _):
             b = n * STEP + i
             at = pl.ds(pl.multiple_of(b * CAP, CAP), CAP)
-            rows = jnp.concatenate([ys[j, at, :] for j in range(4)], axis=0)
+            rows = jnp.concatenate([ys[j, at, :] for j in range(4)] * 2, axis=0)
             outv[b] = lax.dot_general(
                 sel[b], rows, (((0,), (0,)), ((), ())), preferred_element_type=jnp.float32
             ).astype(jnp.bfloat16)
@@ -346,7 +350,7 @@
             pltpu.VMEM((CHIPS * 8, TOK), jnp.float32),
             pltpu.VMEM((CHIPS * 8, TOK), jnp.float32),
             pltpu.VMEM((CHIPS * 8, TOK), jnp.float32),
-            pltpu.VMEM((CHIPS, 4 * CAP, TOK), jnp.bfloat16),
+            pltpu.VMEM((CHIPS, 8 * CAP, TOK), jnp.bfloat16),
             pltpu.VMEM((CHIPS, TOK, D), jnp.bfloat16),
             pltpu.SemaphoreType.DMA((nchunk,)),
             pltpu.SemaphoreType.DMA((8,)),
@@ -504,20 +508,23 @@
         [tiles_of(a) for a in state] + [jnp.zeros((2, 64 * CHUNK - TILES, 8, 128), jnp.bfloat16)], axis=1
     )
     pooled = pooled.reshape(2, devices, CHUNK * 8, 128).transpose(1, 0, 2, 3)
-    spread = lax.all_to_all(pooled, "exp", split_axis=0, concat_axis=0, tiled=True)
-
     share = route_weights / jnp.sum(route_weights, axis=1, keepdims=True)
     meta = jnp.concatenate(
         [
             expert_ids.T.astype(jnp.bfloat16),
             share.T.astype(jnp.bfloat16),
-            jnp.zeros((META, D - 2 * TOK), jnp.bfloat16),
+            (share.T - lax.reduce_precision(share.T, 8, 7)).astype(jnp.bfloat16),
+            jnp.zeros((META, D - 3 * TOK), jnp.bfloat16),
         ],
         axis=1,
     )
-    g, gi, go = gather(96, jnp.concatenate([tokens, meta], axis=0), w_in, w_out)
-
-    picked = jnp.take(spread.reshape(slots, CHUNK * 8, 128), source, axis=0)
+    sent, pooled_in = lax.optimization_barrier((jnp.concatenate([tokens, meta], axis=0), pooled))
+    spread = lax.all_to_all(pooled_in, "exp", split_axis=0, concat_axis=0, tiled=True)
+    g, gi, go = gather(GATHER_ROWS, sent, w_in, w_out)
+    spread, g = lax.optimization_barrier((spread, g))
+
+    picked = jnp.take(spread.reshape(slots, CHUNK * 8, 128), source, axis=0, mode="clip")
+    picked, g = lax.optimization_barrier((picked, g))
     landed = lax.all_to_all(
         picked.reshape(devices, 2, CHUNK * 8, 128), "exp", split_axis=0, concat_axis=0, tiled=True
     )
@@ -525,7 +532,7 @@
     earlier = (old_plan[:, None] == old_plan[None, :]) & (slot_index[None, :] < slot_index[:, None])
     computes = jnp.where(jnp.any(earlier, axis=1), -1, old_plan)
     es = lax.dynamic_slice(computes, (lax.axis_index("exp") // 2 * 4,), (4,))
-    mixed = reduce(96, experts_of(es, g, gi, go))
+    mixed = reduce(REDUCE_ROWS, experts_of(es, g, gi, go))
 
     tiles = landed.transpose(1, 0, 2, 3).reshape(2, 64 * CHUNK, 8, 128)
     outs, at = [], 0

time: 265 us -> 234 us (0.88)
  waiting for transfers between devices: 45 us -> 0.01 us
  Pallas kernels: 181 us -> 195 us
    all_to_all x1, waiting for transfers between devices: 45 us -> 0.01 us  [on_device(): lax.all_to_all(pooled_in, 'exp', split_axis=0, concat_axis=0, tiled=True)]
    pallas_call x1, Pallas kernels: 58.9 us -> 67.4 us  [reduce(): pl.pallas_call(functools.partial(reduce_kernel, pr), out_shape=jax.ShapeD...]
    pallas_call x1, Pallas kernels: 97.2 us -> 103 us  [gather(): pl.pallas_call(functools.partial(gather_kernel, pr), out_shape=(jax.Shape...]
    select_n x2 -> x0, other arithmetic: 3 us -> none  [on_device(): picked = jnp.take(spread.reshape(slots, CHUNK * 8, 128), source, axis=0)]
  transfers between devices with their start and end apart: 2 -> 2, of which waited for: 1 -> 0; matrix products, arithmetic and copies ran while one was open for 1% -> 0% of each run, Pallas kernels for 69% -> 84%
where the time goes in v2:
time: 234 us
  Pallas kernels  195 us (83%)
  starting transfers between devices  22.8 us (10%)
  local copies, waits for them, and re-layouts  10.8 us (5%)
  other arithmetic  3.94 us (2%)
    pallas_call x1, Pallas kernels, gather(): pl.pallas_call(functools.partial(gather_kernel, pr), out_shape=(jax.Shape...  103 us
    pallas_call x1, Pallas kernels, reduce(): pl.pallas_call(functools.partial(reduce_kernel, pr), out_shape=jax.ShapeD...  67.4 us
    pallas_call x1, Pallas kernels, experts_of(): pl.pallas_call(expert_kernel, out_shape=jax.ShapeDtypeStruct((CHIPS, TOK,...  24.6 us
    all_to_all x1, starting transfers between devices, on_device(): lax.all_to_all(pooled_in, 'exp', split_axis=0, concat_axis=0, tiled=True)  15 us
    all_to_all x1, starting transfers between devices, on_device(): lax.all_to_all(picked.reshape(devices, 2, CHUNK * 8, 128), 'exp', split_a...  7.8 us
  transfers between devices with their start and end apart: 2, of which 0 were waited for; matrix products, arithmetic and copies ran while one was open for 0% of the time, Pallas kernels for 84%

profile of v2, /device:TPU:1, one launch (start us, length us, event | category | flops | bytes accessed | tf_op | source)
XLA Modules:
  0.0 233.7 jit_solution(3843214290503811942)
XLA Ops:
  0.6 0.0 copy-start.1
  0.6 0.0 copy-start.2
  0.7 0.8 reduce_sum.9
  1.4 0.7 fusion.2
  2.1 0.7 bitcast_convert_fusion
  2.8 0.7 convert_bitcast_fusion
  3.5 1.0 constant_dynamic-update-slice_fusion.3
  4.5 1.0 constant_dynamic-update-slice_fusion.2
  5.5 1.2 constant_dynamic-update-slice_fusion.1
  6.7 0.0 copy-done.1
  6.7 0.1 constant_dynamic-update-slice_fusion
  6.8 0.0 copy-done.2
  6.8 0.7 maximum_maximum_fusion.xt
  7.6 1.4 copy.18
  9.0 0.0 copy-start.3
  9.0 0.0 copy-start.4
  9.0 15.0 %all-to-all-start = ((bf16[64,2,56,128]{3,2,1,0:T(8,128)(2,1)}), bf16[64,2,56,128]{3,2,1,0:T(8,128)(2,1)S(1)}, u32[]{:S(2)}, u32[]{:S(2)}) async-start(bf16[64,2,56,128]{3,2,1,0:T(8,128)(2,1)} %copy.18), calls=%async_computation | async-start | bytes 3670016 | tf_op jit(solution)/shard_map/all_to_all | solution.py:522
  24.0 103.4 %gather.8 = (bf16[32,136,1024]{2,1,0:T(8,128)(2,1)}, bf16[4,1024,768]{2,1,0:T(8,128)(2,1)}, bf16[4,384,1024]{2,1,0:T(8,128)(2,1)}) custom-call(bf16[136,1024]{1,0:T(8,128)(2,1)} %maximum_maximum_fusion.xt, bf16[2,128,768]{2,1,0:T(8,128)(2,1)} %wi.1, bf16[2,48,1024]{2,1,0:T(8,128)(2,1)} %wo.1), custom_call_target="tpu_custom_call" | custom-call | bytes 200000000 | tf_op jit(solution)/shard_map/gather/pallas_call | solution.py:224
  127.4 0.0 copy-done.3
  127.4 0.0 copy-done.4
  127.4 0.2 select_reduce_fusion
  127.6 0.0 all-to-all-done
  127.6 2.1 gather_fusion
  129.7 7.8 %all-to-all-start.1 = ((bf16[64,2,56,128]{3,2,1,0:T(8,128)(2,1)}), bf16[64,2,56,128]{3,2,1,0:T(8,128)(2,1)S(1)}, u32[]{:S(2)}, u32[]{:S(2)}) async-start(bf16[64,2,56,128]{3,2,1,0:T(8,128)(2,1)} %bitcast.53), calls=%async_computation.1 | async-start | bytes 3670016 | tf_op jit(solution)/shard_map/all_to_all | solution.py:528
  137.5 0.2 fusion.1
  137.7 0.6 dynamic_slice.3.es
  138.3 24.6 %experts.1.part = bf16[32,128,1024]{2,1,0:T(8,128)(2,1)} custom-call(s32[4]{0:T(128)} %dynamic_slice.3.es, bf16[32,136,1024]{2,1,0:T(8,128)(2,1)} %get-tuple-element.19.g, bf16[4,1024,768]{2,1,0:T(8,128)(2,1)} %get-tuple-element.20.wi, bf16[4,384,1024]{2,1,0:T(8,128)(2,1)} %get-tuple-element.21.wo), custom_call_target="tpu_custom_call" | custom-call | flops 6000000000 | bytes 40000000 | tf_op jit(solution)/shard_map/experts/pallas_call | solution.py:339
  162.8 67.4 %reduce.1 = bf16[128,1024]{1,0:T(8,128)(2,1)} custom-call(bf16[32,128,1024]{2,1,0:T(8,128)(2,1)} %experts.1.part), custom_call_target="tpu_custom_call" | custom-call | bytes 200000000 | tf_op jit(solution)/shard_map/reduce/pallas_call | solution.py:464
  230.3 0.0 all-to-all-done.1
  230.3 0.1 copy.19
  230.4 0.0 copy-start
  230.4 0.7 slice.19
  231.1 0.9 slice.20
  232.1 0.9 fusion.3
  233.0 0.0 copy-done
  233.0 0.7 copy.25
  (4 shorter events, 0.0 us)
Async XLA Ops:
  0.6 6.1 %copy-start.1 = (bf16[2,2,48,1024]{3,2,1,0:T(8,128)(2,1)S(1)}, bf16[2,2,48,1024]{3,2,1,0:T(8,128)(2,1)}, u32[]{:S(2)}) copy-start(bf16[2,2,48,1024]{3,2,1,0:T(8,128)(2,1)} %param.13) | copy-start | bytes 1179652
  0.6 6.2 %copy-start.2 = (bf16[128,1024]{1,0:T(8,128)(2,1)S(1)}, bf16[128,1024]{1,0:T(8,128)(2,1)}, u32[]{:S(2)}) copy-start(bf16[128,1024]{1,0:T(8,128)(2,1)} %param.9) | copy-start | bytes 786436
  9.0 118.4 %copy-start.3 = (s32[128]{0:T(128)S(1)}, s32[128]{0:T(128)}, u32[]{:S(2)}) copy-start(s32[128]{0:T(128)} %param.17) | copy-start | bytes 1540
  9.0 118.4 %copy-start.4 = (s32[128]{0:T(128)S(1)}, s32[128]{0:T(128)}, u32[]{:S(2)}) copy-start(s32[128]{0:T(128)} %param.16) | copy-start | bytes 1540
  9.0 118.6 %all-to-all-start = ((bf16[64,2,56,128]{3,2,1,0:T(8,128)(2,1)}), bf16[64,2,56,128]{3,2,1,0:T(8,128)(2,1)S(1)}, u32[]{:S(2)}, u32[]{:S(2)}) async-start(bf16[64,2,56,128]{3,2,1,0:T(8,128)(2,1)} %copy.18), calls=%async_computation | async-start | bytes 3670016 | tf_op jit(solution)/shard_map/all_to_all | solution.py:522
  129.7 100.6 %all-to-all-start.1 = ((bf16[64,2,56,128]{3,2,1,0:T(8,128)(2,1)}), bf16[64,2,56,128]{3,2,1,0:T(8,128)(2,1)S(1)}, u32[]{:S(2)}, u32[]{:S(2)}) async-start(bf16[64,2,56,128]{3,2,1,0:T(8,128)(2,1)} %bitcast.53), calls=%async_computation.1 | async-start | bytes 3670016 | tf_op jit(solution)/shard_map/all_to_all | solution.py:528
  230.4 2.6 %copy-start = (bf16[128,1024]{1,0:T(8,128)(2,1)S(1)}, bf16[128,1024]{1,0:T(8,128)(2,1)}, u32[]{:S(2)}) copy-start(bf16[128,1024]{1,0:T(8,128)(2,1)} %reduce.1) | copy-start | bytes 786436

commit v3 on v0

v3 whole, which is shorter than its diff:
```python
import functools
import heapq

import jax
import jax.numpy as jnp
from jax import lax
from jax.experimental import pallas as pl
from jax.experimental.pallas import tpu as pltpu
from jax.sharding import PartitionSpec as P

TOP = 8
TOK = 128
D = 1024
H = 384
NX, NZ, NY = 4, 8, 8
META = 8
ROWS = TOK + META
CAP = 16
CHIPS = NX * NZ
MESH = pl.DeviceIdType.MESH
VMEM_LIMIT = 63 * 1024 * 1024
TILES = 432
CHUNK = 14
PIECE = CHUNK * 8
GATHER_ROWS = 104
REDUCE_ROWS = 96
AHEAD = 6000.0
RATE = 43.3
HOP = 1500.0
GROUPS = (0, 1, 7, 2, 6, 3, 5, 4)
SPREAD = (4, 3, 5, 2, 6, 1, 7, 0)
TORUS = (("x", 1), ("x", -1), ("z", 1), ("z", -1))
LINKS = TORUS + (("y", 1), ("y", -1), ("c", 0))


def order_of(items):
    after, missing, tail = {n: [] for n in items}, {}, {}
    for name, (_, _, deps) in items.items():
        missing[name] = len(set(deps))
        for d in set(deps):
            after[d].append(name)

    def lag(name):
        axis = items[name][0][0]
        return 0.0 if axis == "t" else 500.0 if axis == "c" else HOP

    def measure(name):
        if name not in tail:
            later = max([measure(n) for n in after[name]], default=0.0)
            tail[name] = items[name][1] + lag(name) + later
        return tail[name]

    place_of = {name: i for i, name in enumerate(items)}
    ready = {item[0][:2]: [] for item in items.values()}
    free, heap, ops, busy = dict.fromkeys(ready, 0.0), [], [], [False]

    def push(name):
        heapq.heappush(ready[items[name][0][:2]], (-measure(name), place_of[name], name))

    def issue(now):
        for link, queue in ready.items():
            while queue and (not busy[0] if link[0] == "t" else free[link] - now < AHEAD):
                name = heapq.heappop(queue)[2]
                busy[0] = busy[0] or link[0] == "t"
                free[link] = max(now, free[link]) + items[name][1]
                heapq.heappush(heap, (free[link] + lag(name), len(ops), name))
                ops.append(("start", name))

    for name in items:
        if not missing[name]:
            push(name)
    now = 0.0
    issue(now)
    while heap:
        now, _, name = heapq.heappop(heap)
        if items[name][0][0] == "t":
            busy[0] = False
        else:
            ops.append(("wait", name))
        for later in after[name]:
            missing[later] -= 1
            if not missing[later]:
                push(later)
        issue(now)
    return ops, now


def split(lo, hi, s):
    mid = lo + ((hi - lo) // 2 + 7) // 8 * 8
    return (lo, mid) if s > 0 else (mid, hi)


def ring(kind, at):
    size = NX if kind[0][1] == "X" else NZ
    at, half = at % size, size // 2
    if at == 0:
        return []
    if at == half:
        return [kind + (1, half), kind + (-1, half)]
    return [kind + (-1, at)] if at < half else [kind + (1, size - at)]


def plan(stage):
    items, span = {}, {}

    def copy(name, link, count, deps):
        items[name] = (link, count / (600.0 if link[0] == "c" else RATE), deps)

    def rows(name, link, lo, hi, deps):
        span[name] = (lo, hi)
        copy(name, link, (hi - lo) * D * 2, deps)

    def step(name, time, deps):
        items[name] = (("t", 0), time, deps)

    pr = GATHER_ROWS
    for s in (1, -1):
        for d in (1, 2, 3, 4):
            lo, hi = split(0, pr, s) if d == 4 else (0, pr)
            rows(("PZ", s, d), ("z", s), lo, hi, [("PZ", s, d - 1)] if d > 1 else [])
        for d in (1, 2):
            lo, hi = split(pr, ROWS, s) if d == 2 else (pr, ROWS)
            rows(("QX", s, d), ("x", s), lo, hi, [("QX", s, 1)] if d > 1 else [])
    for s in (1, -1):
        for d in (1, 2, 3, 4):
            for kind, count in (("WI", 393216), ("WO", 196608)):
                deps = [(kind, s, d - 1)] if d > 1 else []
                copy((kind, s, d), ("y", s), count // (2 if d == 4 else 1), deps)
    for dz in GROUPS:
        for s in (1, -1):
            rows(("PX", dz, s, 1), ("x", s), 0, pr, ring(("PZ",), dz))
            rows(("PX", dz, s, 2), ("x", s), *split(0, pr, s), [("PX", dz, s, 1)])
    for dx in (0, 1, 3, 2):
        for s in (1, -1):
            for d in (1, 2, 3, 4):
                lo, hi = split(pr, ROWS, s) if d == 4 else (pr, ROWS)
                deps = [("QZ", dx, s, d - 1)] if d > 1 else ring(("QX",), dx)
                rows(("QZ", dx, s, d), ("z", s), lo, hi, deps)
    weights = []
    for dy in range(NY):
        for kind, count in (("WI", 393216), ("WO", 196608)):
            copy(("S" + kind, dy), ("c", 0), count, ring((kind + "Y",), dy) and [
                (kind,) + k[1:] for k in ring((kind + "Y",), dy)
            ])
            weights += [("S" + kind, dy)] + items[("S" + kind, dy)][2]

    piece = 2 * PIECE * 128 * 2

    def exchange(tag, after):
        for s in (1, -1):
            copy((tag + "X", s, 2, 1), ("x", s), 4 * piece, after)
            copy((tag + "X", s, 1, 1), ("x", s), 8 * piece, after)
            copy((tag + "X", s, 2, 2), ("x", s), 4 * piece, [(tag + "X", s, 2, 1)])
        ends = [(tag + "X", s, d, d) for s in (1, -1) for d in (1, 2)]
        step(("own", tag), 800.0, ends + after)
        for h in (1, 2, 3, 4):
            for d in (4, 3, 2, 1):
                for s in (1, -1):
                    if d >= h:
                        deps = [(tag + "Z", s, d, h - 1)] if h > 1 else [("own", tag)]
                        copy((tag + "Z", s, d, h), ("z", s), (2 if d == 4 else 4) * piece, deps)
        return [(tag + "Z", s, d, d) for s in (1, -1) for d in (1, 2, 3, 4)]

    ends = exchange("U", [])
    for dz in range(NZ):
        deps = [k + (k[2],) for k in ring(("UZ",), dz)]
        copy(("SU", dz), ("c", 0), 4 * piece, deps or [("own", "U")])

    for dz in SPREAD:
        step(("sum", dz), 300.0, [])

    pr = REDUCE_ROWS

    def fold(name, dz):
        step(("fold", name), 60.0 + 3.0 * (span[name][1] - span[name][0]), [name, ("sum", dz % NZ)])

    for dz in SPREAD:
        for s in (1, -1):
            rows(("A", dz, s), ("x", s), *split(0, pr, s), [("sum", dz)])
            fold(("A", dz, s), dz)
        if dz == 4:
            for dx in (2, 1, 3, 0):
                for s in (1, -1):
                    rows(("D", dx, s, 4), ("z", s), *split(pr, TOK, s), [("sum", 4)])
                    fold(("D", dx, s, 4), 3 * s)
    for dx in (2, 1, 3, 0):
        for s in (1, -1):
            for d in (3, 2, 1):
                deps = [("fold", ("D", dx, s, d + 1)), ("sum", (s * d) % NZ)]
                rows(("D", dx, s, d), ("z", s), pr, TOK, deps)
                fold(("D", dx, s, d), s * (d - 1))
    for s in (1, -1):
        for d in (2, 1):
            dx = (s * d) % NX
            deps = [("fold", ("D", dx, 1, 1)), ("fold", ("D", dx, -1, 1))]
            deps += [("fold", ("E", s, 2))] if d < 2 else []
            rows(("E", s, d), ("x", s), *(split(pr, TOK, s) if d == 2 else (pr, TOK)), deps)
            fold(("E", s, d), 0)
    for dz in SPREAD:
        for s in (1, -1):
            rows(("B", dz, s), ("x", s), 0, pr, [("fold", ("A", dz, s)), ("sum", dz)])
            fold(("B", dz, s), dz)
    for s in (1, -1):
        for d in (4, 3, 2, 1):
            dz = (s * d) % NZ
            deps = [("fold", ("B", dz, 1)), ("fold", ("B", dz, -1))]
            deps += [("fold", ("C", s, d + 1))] if d < 4 else []
            rows(("C", s, d), ("z", s), *(split(0, pr, s) if d == 4 else (0, pr)), deps)
            fold(("C", s, d), s * (d - 1))
    first = {
        name: item for name, item in items.items()
        if name[0][0] in "PQWSU" or name == ("own", "U")
    }
    first = {n: (link, t, [d for d in deps if d in first]) for n, (link, t, deps) in first.items()}
    rest = {n: item for n, item in items.items() if n not in first}
    rest = {n: (link, t, [d for d in deps if d in rest]) for n, (link, t, deps) in rest.items()}
    return first if stage == 0 else rest, span


def gather_kernel(xt, wi, wo, pool, g, gi, go, store, xb, zt, hop, ssem, rsem, lsem):
    run(0, xt, wi, wo, pool, None, g, gi, go, None, None, store, xb, zt, hop, ssem, rsem, lsem, None)


def reduce_kernel(psrc, out, part, land, ssem, rsem, lsem):
    run(1, None, None, None, None, out, None, None, None, part, land, None, None, None, None,
        ssem, rsem, lsem, psrc)


def run(
    stage, xt, wi, wo, pool, out, g, gi, go, part, land, store, xb, zt, hop, ssem, rsem, lsem, psrc,
):
    y = lax.axis_index("grp")
    e = lax.axis_index("exp")
    c = lax.rem(e, 2)
    x, z = e // (2 * NZ), lax.rem(e // 2, NZ)
    xat = [x] + [lax.rem(x + d, NX) for d in range(1, NX)]
    zat = [z] + [lax.rem(z + d, NZ) for d in range(1, NZ)]
    yat = [y] + [lax.rem(y + d, NY) for d in range(1, NY)]
    chips = [[xat[dx] * NZ + zat[dz] for dz in range(NZ)] for dx in range(NX)]
    peer = {("c", 0): (y, e + 1 - 2 * c)}
    for s in (1, -1):
        peer[("x", s)] = (y, 2 * chips[s % NX][0] + c)
        peer[("z", s)] = (y, 2 * chips[0][s % NZ] + c)
        peer[("y", s)] = (yat[s % NY], e)
    span_at = {
        "I": [pl.multiple_of(yat[d] * 128, 128) for d in range(NY)],
        "O": [pl.multiple_of(yat[d] * 48, 16) for d in range(NY)],
    }
    other = 1 - c
    chips_row = [xat[dx] * NZ for dx in range(NX)]
    first_slot = [2 * c, 2 * c + 1, 2 * (1 - c)]

    def chip_at(dx, dz):
        return chips[dx % NX][dz % NZ]

    items, span = plan(stage)
    order, _ = order_of(items)
    copies = [name for name, item in items.items() if item[0][0] != "t"]
    index = {name: i for i, name in enumerate(copies)}
    base, top = {}, 0
    for name in copies:
        if name[0] in ("A", "B", "C", "D", "E"):
            base[name] = top
            top += span[name][1] - span[name][0]
    transit, top = {}, {"U": 0, "V": 0}
    for name in copies:
        if name[0] in ("UZ", "VZ") and name[2] != name[3]:
            transit[name] = top[name[0][0]]
            top[name[0][0]] += 2 if name[2] == 4 else 4
    hop_x = {("U", 1): 0, ("U", -1): 1, ("V", 1): 0, ("V", -1): 1}

    own = chip_at(0, 0)
    def weights(kind, dy, slots, mine):
        ref, size = (gi, 128) if kind == "WI" else (go, 48)
        first = first_slot[slots[0]] if mine else first_slot[2]
        return ref.at[pl.ds(first, slots[1]), pl.ds(span_at[kind[1]][dy % NY], size)]

    links = LINKS if stage == 0 else TORUS
    pending = {}
    if stage == 0:
        pending["last"] = [
            pltpu.make_async_copy(xt, g.at[own], lsem.at[0]),
            pltpu.make_async_copy(wi, weights("WI", 0, (0, 2), 1), lsem.at[1]),
            pltpu.make_async_copy(wo, weights("WO", 0, (0, 2), 1), lsem.at[2]),
        ]
        pending["own", "U"] = [pltpu.make_async_copy(pool.at[pl.ds(chips_row[0], NZ)], xb.at[x], lsem.at[3])]
    else:
        for n, dz in enumerate(SPREAD):
            pending["sum", dz] = [
                pltpu.make_async_copy(psrc.at[chip_at(dx, dz)], part.at[chip_at(dx, dz)], lsem.at[NX * n + dx])
                for dx in range(NX)
            ]
    for group in pending.values():
        for item in group:
            item.start()
    barrier = pltpu.get_barrier_semaphore()
    for link in links:
        pl.semaphore_signal(barrier, inc=1, device_id=peer[link], device_id_type=MESH)
    pl.semaphore_wait(barrier, len(links))

    def block(name, shift):
        kind, s = name[0], name[2] if name[0] in "ABD" else name[1]
        if kind == "A":
            return chip_at(s * (2 - shift), name[1])
        if kind == "B":
            return chip_at(s * (1 - shift), name[1])
        d = name[-1] - shift
        if kind == "C":
            return chip_at(0, s * d)
        if kind == "D":
            return chip_at(name[1], s * d)
        return chip_at(s * d, 0)

    def ends(name, me):
        kind = name[0]
        if kind == "SU":
            at = pl.ds(zat[name[1]], 1)
            return store.at[0, :, at], store.at[1, :, at]
        if kind in ("SWI", "SWO"):
            dst = weights(kind[1:], name[1], (0, 2), me)
            return ((wi if kind == "SWI" else wo) if name[1] == 0 else dst), dst
        if kind in ("WI", "WO"):
            s, d = name[1:]
            slots = (0, 2) if d < 4 else ((0, 1) if s > 0 else (1, 1))
            dst = weights(kind, -s * (d - me), slots, 1)
            if d > 1:
                return dst, dst
            return (wi if kind == "WI" else wo), dst
        if kind in ("UX", "VX"):
            _, s, d, h = name
            half = hop_x[(kind[0], s)]
            first, count = (0, NZ) if d == 1 else ((0, 4) if s > 0 else (4, 4))
            if h == 1:
                frm = pool.at[pl.ds(chips_row[(s * d) % NX] + first, count)]
                if d == 2:
                    return frm, hop.at[pl.ds(4 * half, 4)]
            else:
                frm = hop.at[pl.ds(4 * half, 4)]
            return frm, xb.at[xat[-s * (h - me) % NX], pl.ds(first, count)]
        if kind in ("UZ", "VZ"):
            _, s, d, h = name
            first, count = (0, 4) if d < 4 else ((0, 2) if s > 0 else (2, 2))
            if h == 1:
                frm = xb.at[pl.ds(first, count), pl.ds(zat[s * d % NZ], 1)]
            else:
                frm = zt.at[pl.ds(transit[(kind, s, d, h - 1)], count)]
            if h < d:
                return frm, zt.at[pl.ds(transit[name], count)]
            began = pl.ds(zat[-s * (h - me) % NZ], 1)
            if kind == "UZ":
                return frm, store.at[0, pl.ds(first, count), began]
            raise ValueError(kind)
        lo, hi = span[name]
        if kind in ("A", "B", "C", "D", "E"):
            return part.at[block(name, 0), pl.ds(lo, hi - lo)], land.at[pl.ds(base[name], hi - lo)]
        s, d = name[-2:]
        off = -s * (d - me)
        dx, dz = {"PZ": (0, off), "QX": (off, 0), "PX": (off, name[1]), "QZ": (name[1], off)}[kind]
        dst = g.at[chip_at(dx, dz), pl.ds(lo, hi - lo)]
        mine = me == 1 and dx % NX == 0 and dz % NZ == 0
        return (xt.at[pl.ds(lo, hi - lo)] if mine else dst), dst

    def remote(name, me):
        src, dst = ends(name, me)
        i = index[name]
        return pltpu.make_async_remote_copy(
            src_ref=src if me else dst,
            dst_ref=dst,
            send_sem=ssem.at[i],
            recv_sem=rsem.at[i],
            device_id=peer[items[name][0]],
            device_id_type=MESH,
        )

    def fold(name):
        lo, hi = span[name]
        b = block(name, 1)

        def body(i, _):
            to = pl.ds(pl.multiple_of(lo + i * 16, 16), 16)
            src = pl.ds(pl.multiple_of(base[name] + i * 16, 16), 16)
            part[b, to, :] = (
                part[b, to, :].astype(jnp.float32) + land[src, :].astype(jnp.float32)
            ).astype(jnp.bfloat16)
            return 0

        lax.fori_loop(0, (hi - lo) // 16, body, 0)

    def keep(tag):
        at = pl.ds(zat[0], 1)
        item = pltpu.make_async_copy(xb.at[:, at], store.at[0, :, at], lsem.at[4])
        item.start()
        item.wait()

    for op, name in order:
        if op == "wait":
            remote(name, 0).wait_recv()
        elif items[name][0][0] != "t":
            remote(name, 1).start()
        elif name[0] == "fold":
            fold(name[1])
        else:
            for item in pending.pop(name):
                item.wait()
            if name[0] == "own":
                keep(name[1])
    for item in pending.pop("last", []):
        item.wait()
    if stage:
        out[...] = part[own]
    for name in copies:
        remote(name, 1).wait_send()


PAIR = (2, PIECE, 128)


def semaphores(stage):
    count = sum(1 for item in plan(stage)[0].values() if item[0][0] != "t")
    return [
        pltpu.SemaphoreType.DMA((count,)),
        pltpu.SemaphoreType.DMA((count,)),
        pltpu.SemaphoreType.DMA((CHIPS,)),
    ]


def params_of(stage):
    return pltpu.CompilerParams(
        collective_id=stage, has_side_effects=True, vmem_limit_bytes=VMEM_LIMIT
    )


COST = pl.CostEstimate(flops=0, bytes_accessed=200_000_000, transcendentals=0)
SHAPES = ((CHIPS, ROWS, D), (4, D, 2 * H), (4, H, D))


def gather(xt, wi, wo, pool):
    vmem, anywhere = pl.BlockSpec(memory_space=pltpu.VMEM), pl.BlockSpec(memory_space=pl.ANY)
    return pl.pallas_call(
        gather_kernel,
        out_shape=[jax.ShapeDtypeStruct(n, jnp.bfloat16) for n in SHAPES + ((2, NX, NZ) + PAIR,)],
        in_specs=[vmem, vmem, vmem, anywhere],
        out_specs=[anywhere] * 4,
        scratch_shapes=[
            pltpu.VMEM((NX, NZ) + PAIR, jnp.bfloat16),
            pltpu.VMEM((36, 1) + PAIR, jnp.bfloat16),
            pltpu.VMEM((8,) + PAIR, jnp.bfloat16),
        ]
        + semaphores(0),
        compiler_params=params_of(0),
        cost_estimate=COST,
        name="gather",
    )(xt, wi, wo, pool)


def reduce(part):
    span = plan(1)[1]
    landing = sum(hi - lo for name, (lo, hi) in span.items() if name[0] in ("A", "B", "C", "D", "E"))
    return pl.pallas_call(
        reduce_kernel,
        out_shape=jax.ShapeDtypeStruct((TOK, D), jnp.bfloat16),
        in_specs=[pl.BlockSpec(memory_space=pl.ANY)],
        out_specs=pl.BlockSpec(memory_space=pltpu.VMEM),
        scratch_shapes=[
            pltpu.VMEM((CHIPS, TOK, D), jnp.bfloat16),
            pltpu.VMEM((landing, D), jnp.bfloat16),
        ]
        + semaphores(1),
        compiler_params=params_of(1),
        cost_estimate=COST,
        name="reduce",
    )(part)


STEP = 8


def expert_kernel(es, g, wi, wo, part, gv, wiv, wov, xs, ys, cnt, wgt, rank, sel, outv, isem, wsem, osem):
    nchunk = CHIPS // STEP
    for n in range(nchunk):
        pltpu.make_async_copy(g.at[pl.ds(n * STEP, STEP)], gv.at[pl.ds(n * STEP, STEP)], isem.at[n]).start()
    for j in range(4):
        pltpu.make_async_copy(wi.at[j], wiv.at[j], wsem.at[j]).start()
        pltpu.make_async_copy(wo.at[j], wov.at[j], wsem.at[4 + j]).start()
    tri = (
        lax.broadcasted_iota(jnp.int32, (TOK, TOK), 0) <= lax.broadcasted_iota(jnp.int32, (TOK, TOK), 1)
    ).astype(jnp.bfloat16)
    line = lax.broadcasted_iota(jnp.int32, (CAP, TOK), 0).astype(jnp.float32)
    experts = [es[j].astype(jnp.float32) for j in range(4)]
    for n in range(nchunk):
        pltpu.make_async_copy(
            g.at[pl.ds(n * STEP, STEP)], gv.at[pl.ds(n * STEP, STEP)], isem.at[n]
        ).wait()

        def count(i, _):
            b = n * STEP + i
            meta = gv[b, TOK:ROWS, 0 : 3 * TOK].astype(jnp.float32)
            ids, share = meta[:, 0:TOK], meta[:, TOK : 2 * TOK] + meta[:, 2 * TOK :]
            named = [ids == experts[j] for j in range(4)]
            ones = [jnp.sum(jnp.where(m, 1.0, 0.0), axis=0, keepdims=True) for m in named]
            held = [jnp.sum(jnp.where(m, share, 0.0), axis=0, keepdims=True) for m in named]
            rows = pl.ds(pl.multiple_of(b * 8, 8), 8)
            cnt[rows, :] = jnp.concatenate(ones + ones, axis=0)
            wgt[rows, :] = jnp.concatenate(held + held, axis=0)
            return 0

        lax.fori_loop(0, STEP, count, 0)
        rows = pl.ds(n * STEP * 8, STEP * 8)
        chosen = cnt[rows, :]
        upto = jnp.dot(chosen.astype(jnp.bfloat16), tri, preferred_element_type=jnp.float32)
        rank[rows, :] = jnp.where(chosen > 0.5, upto - 1.0, -1.0)

        def pick(i, _):
            b = n * STEP + i
            rows = pl.ds(pl.multiple_of(b * 8, 8), 8)
            place8, held8 = rank[rows, :], wgt[rows, :]
            hit = [line == place8[j : j + 1, :] for j in range(4)]
            onehot = jnp.concatenate([jnp.where(m, 1.0, 0.0) for m in hit], axis=0)
            weight = jnp.concatenate(
                [jnp.where(hit[j], held8[j : j + 1, :], 0.0) for j in range(4)], axis=0
            )
            high = weight.astype(jnp.bfloat16)
            sel[b, 0 : 4 * CAP, :] = high
            sel[b, 4 * CAP :, :] = (weight - high.astype(jnp.float32)).astype(jnp.bfloat16)
            got = jnp.dot(
                onehot.astype(jnp.bfloat16), gv[b, 0:TOK, :], preferred_element_type=jnp.float32
            ).astype(jnp.bfloat16)
            at = pl.ds(pl.multiple_of(b * CAP, CAP), CAP)
            for j in range(4):
                xs[j, at, :] = got[j * CAP : (j + 1) * CAP, :]
            return 0

        lax.fori_loop(0, STEP, pick, 0, unroll=2)
    for j in range(4):
        pltpu.make_async_copy(wi.at[j], wiv.at[j], wsem.at[j]).wait()
        pltpu.make_async_copy(wo.at[j], wov.at[j], wsem.at[4 + j]).wait()

    def mlp(i, _):
        j, at = i // 2, pl.ds(pl.multiple_of(lax.rem(i, 2) * 256, 256), 256)
        both = jnp.dot(xs[j, at, :], wiv[j], preferred_element_type=jnp.float32)
        hidden = (jax.nn.silu(both[:, :H]) * both[:, H:]).astype(jnp.bfloat16)
        ys[j, at, :] = jnp.dot(hidden, wov[j], preferred_element_type=jnp.float32).astype(jnp.bfloat16)
        return 0

    lax.fori_loop(0, 8, mlp, 0)
    for n in range(nchunk):

        def spread(i, _):
            b = n * STEP + i
            at = pl.ds(pl.multiple_of(b * CAP, CAP), CAP)
            rows = jnp.concatenate([ys[j, at, :] for j in range(4)] * 2, axis=0)
            outv[b] = lax.dot_general(
                sel[b], rows, (((0,), (0,)), ((), ())), preferred_element_type=jnp.float32
            ).astype(jnp.bfloat16)
            return 0

        lax.fori_loop(0, STEP, spread, 0, unroll=2)
        pltpu.make_async_copy(outv.at[pl.ds(n * STEP, STEP)], part.at[pl.ds(n * STEP, STEP)], osem.at[n]).start()
    for n in range(nchunk):
        pltpu.make_async_copy(
            outv.at[pl.ds(n * STEP, STEP)], part.at[pl.ds(n * STEP, STEP)], osem.at[n]
        ).wait()


def experts_of(es, g, wi, wo):
    any_space = pl.BlockSpec(memory_space=pl.ANY)
    nchunk = CHIPS // STEP
    return pl.pallas_call(
        expert_kernel,
        out_shape=jax.ShapeDtypeStruct((CHIPS, TOK, D), jnp.bfloat16),
        in_specs=[pl.BlockSpec(memory_space=pltpu.SMEM)] + [any_space] * 3,
        out_specs=any_space,
        scratch_shapes=[
            pltpu.VMEM((CHIPS, ROWS, D), jnp.bfloat16),
            pltpu.VMEM((4, D, 2 * H), jnp.bfloat16),
            pltpu.VMEM((4, H, D), jnp.bfloat16),
            pltpu.VMEM((4, CHIPS * CAP, D), jnp.bfloat16),
            pltpu.VMEM((4, CHIPS * CAP, D), jnp.bfloat16),
            pltpu.VMEM((CHIPS * 8, TOK), jnp.float32),
            pltpu.VMEM((CHIPS * 8, TOK), jnp.float32),
            pltpu.VMEM((CHIPS * 8, TOK), jnp.float32),
            pltpu.VMEM((CHIPS, 8 * CAP, TOK), jnp.bfloat16),
            pltpu.VMEM((CHIPS, TOK, D), jnp.bfloat16),
            pltpu.SemaphoreType.DMA((nchunk,)),
            pltpu.SemaphoreType.DMA((8,)),
            pltpu.SemaphoreType.DMA((nchunk,)),
        ],
        compiler_params=pltpu.CompilerParams(vmem_limit_bytes=VMEM_LIMIT),
        cost_estimate=pl.CostEstimate(flops=6_000_000_000, bytes_accessed=40_000_000, transcendentals=0),
        name="experts",
    )(es, g, wi, wo)


def tiles_of(array):
    slots, columns = array.shape[0], array.shape[-1]
    rows = array.size // slots // columns
    tiled = array.reshape(slots, rows // 8, 8, columns // 128, 128)
    return tiled.transpose(0, 1, 3, 2, 4).reshape(slots, -1, 8, 128)


def untile(tiles, shape):
    slots, columns = shape[0], shape[-1]
    tiled = tiles.reshape(slots, -1, columns // 128, 8, 128)
    return tiled.transpose(0, 1, 3, 2, 4).reshape(shape)


def on_device(
    tokens, w_in, w_out, moments_in, moments_out, expert_ids, route_weights, old_plan, new_plan
):
    devices = lax.axis_size("exp")
    slots = 2 * devices
    slot_index = jnp.arange(slots, dtype=jnp.int32)
    same_expert = new_plan[:, None] == old_plan[None, :]
    source = jnp.min(jnp.where(same_expert, slot_index[None, :], slots), axis=1)

    state = [w_in, w_out, moments_in, moments_out]
    pooled = jnp.concatenate(
        [tiles_of(a) for a in state]
        + [jnp.zeros((2, CHIPS * CHUNK - TILES, 8, 128), jnp.bfloat16)],
        axis=1,
    )
    pooled = pooled.reshape(2, CHIPS, PIECE, 128).transpose(1, 0, 2, 3)

    share = route_weights / jnp.sum(route_weights, axis=1, keepdims=True)
    meta = jnp.concatenate(
        [
            expert_ids.T.astype(jnp.bfloat16),
            share.T.astype(jnp.bfloat16),
            (share.T - lax.reduce_precision(share.T, 8, 7)).astype(jnp.bfloat16),
            jnp.zeros((META, D - 3 * TOK), jnp.bfloat16),
        ],
        axis=1,
    )
    earlier = (old_plan[:, None] == old_plan[None, :]) & (slot_index[None, :] < slot_index[:, None])
    computes = jnp.where(jnp.any(earlier, axis=1), -1, old_plan)
    es = lax.dynamic_slice(computes, (lax.axis_index("exp") // 2 * 4,), (4,))
    sent = jnp.concatenate([tokens, meta], axis=0)
    g, gi, go, store = gather(sent, w_in, w_out, pooled)
    core = lax.axis_index("exp") % 2
    row = (source // 2 % 2 != core) * (2 * CHIPS) + source // 4 * 2 + source % 2
    picked = jnp.take(store.reshape(8 * CHIPS, PIECE // 2, 128), 2 * row + core, axis=0, mode="clip")
    picked, g = lax.optimization_barrier((picked, g))
    landed = lax.all_to_all(
        picked.reshape(devices, 2, PIECE // 2, 128), "exp", split_axis=0, concat_axis=0, tiled=True
    )
    mixed = reduce(experts_of(es, g, gi, go))
    tiles = landed.transpose(1, 0, 2, 3)
    tiles = tiles.reshape(2, CHIPS * CHUNK, 8, 128)
    outs, at = [], 0
    for a in state:
        count = a.size // 2 // 1024
        outs.append(untile(tiles[:, at : at + count], a.shape))
        at += count
    return (mixed, *outs)


def solution(mesh):
    return jax.shard_map(
        on_device,
        mesh=mesh,
        in_specs=(
            P(("grp", "exp"), None),
            P("exp", "grp", None),
            P("exp", "grp", None),
            P("exp", None, "grp", None),
            P("exp", None, "grp", None),
            P(("grp", "exp"), None),
            P(("grp", "exp"), None),
            P(),
            P(),
        ),
        out_specs=(
            P(("grp", "exp"), None),
            P("exp", "grp", None),
            P("exp", "grp", None),
            P("exp", None, "grp", None),
            P("exp", None, "grp", None),
        ),
        check_vma=False,
    )
```

time: 433 us -> 220 us (0.51); the launches traced: 428 us -> 219 us
  waiting for transfers between devices: 258 us -> 0.01 us
  Pallas kernels: 0 us -> 192 us
  starting transfers between devices: 83.1 us -> 7.82 us
  local copies, waits for them, and re-layouts: 47 us -> 14.3 us
  matrix products: 18.9 us -> 0 us
  between operations: 14.7 us -> 0.8 us
    all_to_all x10 -> x1, waiting for transfers between devices: 258 us -> 0.01 us  [on_device(): lax.all_to_all(picked.reshape(devices, 2, PIECE // 2, 128), 'exp', split_...]
    pallas_call x0 -> x3, Pallas kernels: none -> 192 us  [the longest x1 98.8 us: gather(): pl.pallas_call(gather_kernel, out_shape=[jax.ShapeDtypeStruct(n, jnp.bflo...]
    all_to_all x10 -> x1, starting transfers between devices: 83 us -> 7.82 us  [on_device(): lax.all_to_all(picked.reshape(devices, 2, PIECE // 2, 128), 'exp', split_...]
    dot_general x2 -> x0, matrix products: 18.9 us -> none  [the longest x1 13.2 us: on_device(): jnp.einsum('njcd,jdh->njch', lax.all_to_all(outgoing, 'exp', split_axis=0...]
    scatter x1 -> x0, local copies, waits for them, and re-layouts: 15.3 us -> none  [on_device(): jnp.zeros((slot_count * capacity, width), jnp.bfloat16).at[target]]
    all_to_all x18 -> x0, local copies, waits for them, and re-layouts: 10.6 us -> none  [the longest x3 2.45 us: on_device(): lax.all_to_all(flat_moments_in, 'exp', split_axis=1, concat_axis=0, tiled...]
    gather x7 -> x1, local copies, waits for them, and re-layouts: 11.8 us -> 4.09 us  [on_device(): jnp.take(store.reshape(8 * CHIPS, PIECE // 2, 128), 2 * row + core, axis=...]
    convert_element_type x1 -> x0, local copies, waits for them, and re-layouts: 4.5 us -> none  [on_device(): result = jnp.einsum('njch,jhd->njcd', hidden, full_out, preferred_element...]
  transfers between devices with their start and end apart: 12 -> 1, of which waited for: 9 -> 0; matrix products, arithmetic and copies ran while one was open for 13% -> 0% of each run, Pallas kernels for 0% -> 42%
where the time goes in v3:
time: 220 us; the launch traced here: 219 us
  Pallas kernels  192 us (87%)
  local copies, waits for them, and re-layouts  14.3 us (6%)
  starting transfers between devices  7.82 us (4%)
  other arithmetic  4.62 us (2%)
    pallas_call x1, Pallas kernels, gather(): pl.pallas_call(gather_kernel, out_shape=[jax.ShapeDtypeStruct(n, jnp.bflo...  98.8 us
    pallas_call x1, Pallas kernels, reduce(): pl.pallas_call(reduce_kernel, out_shape=jax.ShapeDtypeStruct((TOK, D), jn...  68.3 us
    pallas_call x1, Pallas kernels, experts_of(): pl.pallas_call(expert_kernel, out_shape=jax.ShapeDtypeStruct((CHIPS, TOK,...  24.6 us
    all_to_all x1, starting transfers between devices, on_device(): lax.all_to_all(picked.reshape(devices, 2, PIECE // 2, 128), 'exp', split_...  7.82 us
  transfers between devices with their start and end apart: 1, of which 0 were waited for; matrix products, arithmetic and copies ran while one was open for 0% of the time, Pallas kernels for 42%

profile of v3, /device:TPU:1, one launch (start us, length us, event | category | flops | bytes accessed | tf_op | source)
XLA Modules:
  0.0 219.2 jit_solution(18003929563186282027)
XLA Ops:
  0.6 0.0 copy-start.1
  0.6 0.8 reduce_sum.9
  1.4 0.7 fusion.2
  2.1 0.7 bitcast_convert_fusion
  2.8 0.7 convert_bitcast_fusion
  3.5 0.8 select_reduce_fusion
  4.4 1.0 constant_dynamic-update-slice_fusion.3
  5.4 1.0 constant_dynamic-update-slice_fusion.2
  6.4 1.2 constant_dynamic-update-slice_fusion.1
  7.6 0.0 copy-done.1
  7.6 0.1 constant_dynamic-update-slice_fusion
  7.7 0.0 copy-start.2
  7.7 1.4 copy_bitcast_fusion.pool
  9.1 0.0 copy-done.2
  9.1 0.7 maximum_maximum_fusion.xt
  9.9 98.8 %gather.8 = (bf16[32,136,1024]{2,1,0:T(8,128)(2,1)}, bf16[4,1024,768]{2,1,0:T(8,128)(2,1)}, bf16[4,384,1024]{2,1,0:T(8,128)(2,1)}, bf16[2,4,8,2,112,128]{5,4,3,2,1,0:T(8,128)(2,1)}) custom-call(bf16[136,1024]{1,0:T(8,128)(2,1)} %maximum_maximum_fusion.xt, bf16[2,128,768]{2,1,0:T(8,128)(2,1)} %wi.1, bf16[2,48,1024]{2,1,0:T(8,128)(2,1)} %wo.1, ...), custom_call_target="tpu_custom_call" | custom-call | bytes 200000000 | tf_op jit(solution)/shard_map/gather/pallas_call | solution.py:439
  108.7 4.1 %gather_fusion = bf16[128,56,128]{2,1,0:T(8,128)(2,1)} fusion(bf16[256,56,128]{2,1,0:T(8,128)(2,1)} %bitcast.81, s32[1024]{0:T(1024)S(1)} %pad_clamp_fusion), kind=kCustom, calls=%fused_computation | custom fusion | bytes 3670528 | tf_op jit(solution)/shard_map/jit(_take)/gather | solution.py:641
  112.8 0.0 copy-start.3
  112.8 7.8 %all-to-all-start = ((bf16[64,2,56,128]{3,2,1,0:T(8,128)(2,1)}), bf16[64,2,56,128]{3,2,1,0:T(8,128)(2,1)}, u32[]{:S(2)}, u32[]{:S(2)}) async-start(bf16[64,2,56,128]{3,2,1,0:T(8,128)(2,1)} %bitcast.19), calls=%async_computation | async-start | bytes 3670016 | tf_op jit(solution)/shard_map/all_to_all | solution.py:643
  120.6 0.0 copy-done.3
  120.6 0.2 fusion.1
  120.8 0.6 dynamic_slice.3.es
  121.4 24.6 %experts.1.psrc = bf16[32,128,1024]{2,1,0:T(8,128)(2,1)} custom-call(s32[4]{0:T(128)} %dynamic_slice.3.es, bf16[32,136,1024]{2,1,0:T(8,128)(2,1)} %get-tuple-element.13.g, bf16[4,1024,768]{2,1,0:T(8,128)(2,1)} %get-tuple-element.14.wi, bf16[4,384,1024]{2,1,0:T(8,128)(2,1)} %get-tuple-element.15.wo), custom_call_target="tpu_custom_call" | custom-call | flops 6000000000 | bytes 40000000 | tf_op jit(solution)/shard_map/experts/pallas_call | solution.py:568
  146.0 68.3 %reduce.1 = bf16[128,1024]{1,0:T(8,128)(2,1)} custom-call(bf16[32,128,1024]{2,1,0:T(8,128)(2,1)} %experts.1.psrc), custom_call_target="tpu_custom_call" | custom-call | bytes 200000000 | tf_op jit(solution)/shard_map/reduce/pallas_call | solution.py:459
  214.3 0.0 all-to-all-done
  214.3 1.6 copy.18
  215.9 0.0 copy-start
  215.9 0.7 slice.19
  216.6 0.9 slice.20
  217.6 0.9 fusion.6
  218.5 0.0 copy-done
  218.5 0.7 copy.25
  (5 shorter events, 0.1 us)
Async XLA Ops:
  0.6 7.0 %copy-start.1 = (bf16[2,2,48,1024]{3,2,1,0:T(8,128)(2,1)S(1)}, bf16[2,2,48,1024]{3,2,1,0:T(8,128)(2,1)}, u32[]{:S(2)}) copy-start(bf16[2,2,48,1024]{3,2,1,0:T(8,128)(2,1)} %param.13) | copy-start | bytes 1179652
  7.7 1.4 copy-start.2
  112.8 7.9 %copy-start.3 = (s32[128]{0:T(128)S(1)}, s32[128]{0:T(128)}, u32[]{:S(2)}) copy-start(s32[128]{0:T(128)} %param.16) | copy-start | bytes 1540
  112.8 101.5 %all-to-all-start = ((bf16[64,2,56,128]{3,2,1,0:T(8,128)(2,1)}), bf16[64,2,56,128]{3,2,1,0:T(8,128)(2,1)}, u32[]{:S(2)}, u32[]{:S(2)}) async-start(bf16[64,2,56,128]{3,2,1,0:T(8,128)(2,1)} %bitcast.19), calls=%async_computation | async-start | bytes 3670016 | tf_op jit(solution)/shard_map/all_to_all | solution.py:643
  215.9 2.6 %copy-start = (bf16[128,1024]{1,0:T(8,128)(2,1)S(1)}, bf16[128,1024]{1,0:T(8,128)(2,1)}, u32[]{:S(2)}) copy-start(bf16[128,1024]{1,0:T(8,128)(2,1)} %reduce.1) | copy-start | bytes 786436

commit v4 on v3

--- a/solution.py
+++ b/solution.py
@@ -23,8 +23,9 @@
 CHUNK = 14
 PIECE = CHUNK * 8
 GATHER_ROWS = 104
-REDUCE_ROWS = 96
-AHEAD = 6000.0
+REDUCE_ROWS = 80
+AHEAD = 4000.0
+BESIDE = 25000.0
 RATE = 43.3
 HOP = 1500.0
 GROUPS = (0, 1, 7, 2, 6, 3, 5, 4)
@@ -33,7 +34,7 @@
 LINKS = TORUS + (("y", 1), ("y", -1), ("c", 0))
 
 
-def order_of(items):
+def order_of(items, beside=0.0):
     after, missing, tail = {n: [] for n in items}, {}, {}
     for name, (_, _, deps) in items.items():
         missing[name] = len(set(deps))
@@ -62,7 +63,9 @@
             while queue and (not busy[0] if link[0] == "t" else free[link] - now < AHEAD):
                 name = heapq.heappop(queue)[2]
                 busy[0] = busy[0] or link[0] == "t"
-                free[link] = max(now, free[link]) + items[name][1]
+                begin = max(now, free[link])
+                slow = {"z": 2.0, "x": 1.5}.get(link[0], 1.0) if begin < beside else 1.0
+                free[link] = begin + slow * items[name][1]
                 heapq.heappush(heap, (free[link] + lag(name), len(ops), name))
                 ops.append(("start", name))
 
@@ -85,8 +88,8 @@
     return ops, now
 
 
-def split(lo, hi, s):
-    mid = lo + ((hi - lo) // 2 + 7) // 8 * 8
+def split(lo, hi, s, unit=8):
+    mid = lo + -(-(hi - lo) // (2 * unit)) * unit
     return (lo, mid) if s > 0 else (mid, hi)
 
 
@@ -176,12 +179,12 @@
 
     for dz in SPREAD:
         for s in (1, -1):
-            rows(("A", dz, s), ("x", s), *split(0, pr, s), [("sum", dz)])
+            rows(("A", dz, s), ("x", s), *split(0, pr, s, 16), [("sum", dz)])
             fold(("A", dz, s), dz)
         if dz == 4:
             for dx in (2, 1, 3, 0):
                 for s in (1, -1):
-                    rows(("D", dx, s, 4), ("z", s), *split(pr, TOK, s), [("sum", 4)])
+                    rows(("D", dx, s, 4), ("z", s), *split(pr, TOK, s, 16), [("sum", 4)])
                     fold(("D", dx, s, 4), 3 * s)
     for dx in (2, 1, 3, 0):
         for s in (1, -1):
@@ -194,7 +197,7 @@
             dx = (s * d) % NX
             deps = [("fold", ("D", dx, 1, 1)), ("fold", ("D", dx, -1, 1))]
             deps += [("fold", ("E", s, 2))] if d < 2 else []
-            rows(("E", s, d), ("x", s), *(split(pr, TOK, s) if d == 2 else (pr, TOK)), deps)
+            rows(("E", s, d), ("x", s), *(split(pr, TOK, s, 16) if d == 2 else (pr, TOK)), deps)
             fold(("E", s, d), 0)
     for dz in SPREAD:
         for s in (1, -1):
@@ -205,7 +208,7 @@
             dz = (s * d) % NZ
             deps = [("fold", ("B", dz, 1)), ("fold", ("B", dz, -1))]
             deps += [("fold", ("C", s, d + 1))] if d < 4 else []
-            rows(("C", s, d), ("z", s), *(split(0, pr, s) if d == 4 else (0, pr)), deps)
+            rows(("C", s, d), ("z", s), *(split(0, pr, s, 16) if d == 4 else (0, pr)), deps)
             fold(("C", s, d), s * (d - 1))
     first = {
         name: item for name, item in items.items()
@@ -254,7 +257,7 @@
         return chips[dx % NX][dz % NZ]
 
     items, span = plan(stage)
-    order, _ = order_of(items)
+    order, _ = order_of(items, BESIDE if stage else 0.0)
     copies = [name for name, item in items.items() if item[0][0] != "t"]
     index = {name: i for i, name in enumerate(copies)}
     base, top = {}, 0
@@ -504,7 +507,7 @@
             wgt[rows, :] = jnp.concatenate(held + held, axis=0)
             return 0
 
-        lax.fori_loop(0, STEP, count, 0)
+        lax.fori_loop(0, STEP, count, 0, unroll=4)
         rows = pl.ds(n * STEP * 8, STEP * 8)
         chosen = cnt[rows, :]
         upto = jnp.dot(chosen.astype(jnp.bfloat16), tri, preferred_element_type=jnp.float32)
@@ -530,7 +533,7 @@
                 xs[j, at, :] = got[j * CAP : (j + 1) * CAP, :]
             return 0
 
-        lax.fori_loop(0, STEP, pick, 0, unroll=2)
+        lax.fori_loop(0, STEP, pick, 0, unroll=4)
     for j in range(4):
         pltpu.make_async_copy(wi.at[j], wiv.at[j], wsem.at[j]).wait()
         pltpu.make_async_copy(wo.at[j], wov.at[j], wsem.at[4 + j]).wait()
@@ -542,7 +545,7 @@
         ys[j, at, :] = jnp.dot(hidden, wov[j], preferred_element_type=jnp.float32).astype(jnp.bfloat16)
         return 0
 
-    lax.fori_loop(0, 8, mlp, 0)
+    lax.fori_loop(0, 8, mlp, 0, unroll=2)
     for n in range(nchunk):
 
         def spread(i, _):
@@ -554,7 +557,7 @@
             ).astype(jnp.bfloat16)
             return 0
 
-        lax.fori_loop(0, STEP, spread, 0, unroll=2)
+        lax.fori_loop(0, STEP, spread, 0, unroll=4)
         pltpu.make_async_copy(outv.at[pl.ds(n * STEP, STEP)], part.at[pl.ds(n * STEP, STEP)], osem.at[n]).start()
     for n in range(nchunk):
         pltpu.make_async_copy(

time: 220 us -> 217 us (0.986)
    pallas_call x1, Pallas kernels: 24.6 us -> 20.6 us  [experts_of(): pl.pallas_call(expert_kernel, out_shape=jax.ShapeDtypeStruct((CHIPS, TOK,...]
where the time goes in v4:
time: 217 us; the launch traced here: 216 us
  Pallas kernels  190 us (88%)
  local copies, waits for them, and re-layouts  14.3 us (7%)
  starting transfers between devices  6.76 us (3%)
  other arithmetic  4.62 us (2%)
    pallas_call x1, Pallas kernels, gather(): pl.pallas_call(gather_kernel, out_shape=[jax.ShapeDtypeStruct(n, jnp.bflo...  99.9 us
    pallas_call x1, Pallas kernels, reduce(): pl.pallas_call(reduce_kernel, out_shape=jax.ShapeDtypeStruct((TOK, D), jn...  69.6 us
    pallas_call x1, Pallas kernels, experts_of(): pl.pallas_call(expert_kernel, out_shape=jax.ShapeDtypeStruct((CHIPS, TOK,...  20.6 us
    all_to_all x1, starting transfers between devices, on_device(): lax.all_to_all(picked.reshape(devices, 2, PIECE // 2, 128), 'exp', split_...  6.76 us
  transfers between devices with their start and end apart: 1, of which 0 were waited for; matrix products, arithmetic and copies ran while one was open for 0% of the time, Pallas kernels for 42%

profile of v4, /device:TPU:1, one launch (start us, length us, event | category | flops | bytes accessed | tf_op | source)
XLA Modules:
  0.0 216.5 jit_solution(7006343484954490712)
XLA Ops:
  0.6 0.0 copy-start.1
  0.6 0.8 reduce_sum.9
  1.4 0.7 fusion.2
  2.1 0.7 bitcast_convert_fusion
  2.8 0.7 convert_bitcast_fusion
  3.5 0.8 select_reduce_fusion
  4.4 1.0 constant_dynamic-update-slice_fusion.3
  5.4 1.0 constant_dynamic-update-slice_fusion.2
  6.4 1.2 constant_dynamic-update-slice_fusion.1
  7.6 0.0 copy-done.1
  7.6 0.1 constant_dynamic-update-slice_fusion
  7.7 0.0 copy-start.2
  7.7 1.4 copy_bitcast_fusion.pool
  9.1 0.0 copy-done.2
  9.1 0.7 maximum_maximum_fusion.xt
  9.9 99.9 %gather.8 = (bf16[32,136,1024]{2,1,0:T(8,128)(2,1)}, bf16[4,1024,768]{2,1,0:T(8,128)(2,1)}, bf16[4,384,1024]{2,1,0:T(8,128)(2,1)}, bf16[2,4,8,2,112,128]{5,4,3,2,1,0:T(8,128)(2,1)}) custom-call(bf16[136,1024]{1,0:T(8,128)(2,1)} %maximum_maximum_fusion.xt, bf16[2,128,768]{2,1,0:T(8,128)(2,1)} %wi.1, bf16[2,48,1024]{2,1,0:T(8,128)(2,1)} %wo.1, ...), custom_call_target="tpu_custom_call" | custom-call | bytes 200000000 | tf_op jit(solution)/shard_map/gather/pallas_call | solution.py:442
  109.7 4.1 %gather_fusion = bf16[128,56,128]{2,1,0:T(8,128)(2,1)} fusion(bf16[256,56,128]{2,1,0:T(8,128)(2,1)} %bitcast.81, s32[1024]{0:T(1024)S(1)} %pad_clamp_fusion), kind=kCustom, calls=%fused_computation | custom fusion | bytes 3670528 | tf_op jit(solution)/shard_map/jit(_take)/gather | solution.py:644
  113.8 0.0 copy-start.3
  113.8 6.8 %all-to-all-start = ((bf16[64,2,56,128]{3,2,1,0:T(8,128)(2,1)}), bf16[64,2,56,128]{3,2,1,0:T(8,128)(2,1)}, u32[]{:S(2)}, u32[]{:S(2)}) async-start(bf16[64,2,56,128]{3,2,1,0:T(8,128)(2,1)} %bitcast.19), calls=%async_computation | async-start | bytes 3670016 | tf_op jit(solution)/shard_map/all_to_all | solution.py:646
  120.6 0.0 copy-done.3
  120.6 0.2 fusion.1
  120.8 0.6 dynamic_slice.3.es
  121.4 20.6 %experts.1.psrc = bf16[32,128,1024]{2,1,0:T(8,128)(2,1)} custom-call(s32[4]{0:T(128)} %dynamic_slice.3.es, bf16[32,136,1024]{2,1,0:T(8,128)(2,1)} %get-tuple-element.13.g, bf16[4,1024,768]{2,1,0:T(8,128)(2,1)} %get-tuple-element.14.wi, bf16[4,384,1024]{2,1,0:T(8,128)(2,1)} %get-tuple-element.15.wo), custom_call_target="tpu_custom_call" | custom-call | flops 6000000000 | bytes 40000000 | tf_op jit(solution)/shard_map/experts/pallas_call | solution.py:571
  142.0 69.6 %reduce.1 = bf16[128,1024]{1,0:T(8,128)(2,1)} custom-call(bf16[32,128,1024]{2,1,0:T(8,128)(2,1)} %experts.1.psrc), custom_call_target="tpu_custom_call" | custom-call | bytes 200000000 | tf_op jit(solution)/shard_map/reduce/pallas_call | solution.py:462
  211.5 0.0 all-to-all-done
  211.5 1.6 copy.18
  213.2 0.0 copy-start
  213.2 0.7 slice.19
  213.9 0.9 slice.20
  214.8 0.9 fusion.6
  215.8 0.0 copy-done
  215.8 0.7 copy.25
  (5 shorter events, 0.1 us)
Async XLA Ops:
  0.6 7.0 %copy-start.1 = (bf16[2,2,48,1024]{3,2,1,0:T(8,128)(2,1)S(1)}, bf16[2,2,48,1024]{3,2,1,0:T(8,128)(2,1)}, u32[]{:S(2)}) copy-start(bf16[2,2,48,1024]{3,2,1,0:T(8,128)(2,1)} %param.13) | copy-start | bytes 1179652
  7.7 1.4 copy-start.2
  113.8 6.8 %copy-start.3 = (s32[128]{0:T(128)S(1)}, s32[128]{0:T(128)}, u32[]{:S(2)}) copy-start(s32[128]{0:T(128)} %param.16) | copy-start | bytes 1540
  113.8 97.7 %all-to-all-start = ((bf16[64,2,56,128]{3,2,1,0:T(8,128)(2,1)}), bf16[64,2,56,128]{3,2,1,0:T(8,128)(2,1)}, u32[]{:S(2)}, u32[]{:S(2)}) async-start(bf16[64,2,56,128]{3,2,1,0:T(8,128)(2,1)} %bitcast.19), calls=%async_computation | async-start | bytes 3670016 | tf_op jit(solution)/shard_map/all_to_all | solution.py:646
  213.2 2.6 %copy-start = (bf16[128,1024]{1,0:T(8,128)(2,1)S(1)}, bf16[128,1024]{1,0:T(8,128)(2,1)}, u32[]{:S(2)}) copy-start(bf16[128,1024]{1,0:T(8,128)(2,1)} %reduce.1) | copy-start | bytes 786436
